TPU v7x, 32 devices: a whole 2x2x4 slice. The times are simulated.
32 devices in a mesh: groups: 2 (over x), tensor: 4 (over y, core), dp: 4 (over z).
Axes of the slice: x: 2, y: 2, z: 4, core: 2. Of those that a mesh axis runs over, the one named last changes fastest.
Arguments:
- first_out: bfloat16 [4096, 1024], P(('groups', 'tensor', 'dp')), parts along dimension 0, may hold values from -6 to 6
- second_out: bfloat16 [4096, 1024], P(('groups', 'tensor', 'dp')), parts along dimension 0, may hold values from -6 to 6
- grad_first: bfloat16 [4096, 1024], P(('groups', 'tensor', 'dp')), parts along dimension 0, may hold values from -6 to 6
- grad_second: bfloat16 [4096, 1024], P(('groups', 'tensor', 'dp')), parts along dimension 0, may hold values from -6 to 6
- w_up: bfloat16 [1024, 8192], P('dp', 'tensor'), may hold values from -0.1875 to 0.1875
- w_down: bfloat16 [8192, 1024], P('tensor', 'dp'), may hold values from -0.0625 to 0.0625
- norm_gain: float32 [1024], replicated, may hold values from 0.25 to 1.75
- norm_bias: float32 [1024], replicated, may hold values from -3 to 3
Outputs:
- second_in: bfloat16 [4096, 1024], P(('groups', 'tensor', 'dp')), parts along dimension 0
- grad_first_in: float32 [4096, 1024], P(('groups', 'tensor', 'dp')), parts along dimension 0
- grad_up: float32 [2048, 8192], P(('groups', 'dp'), 'tensor'), parts along dimension 0
- grad_down: float32 [16384, 1024], P(('groups', 'tensor'), 'dp'), parts along dimension 0
- grad_norm: float32 [4, 1024], P('groups'), parts along dimension 0
There are 2 independent parts, one for each index of `groups`. A program takes and returns all parts, laid end to end along the dimension named above; an argument that names none is the same for every part. Nothing has to cross between parts.
All inputs are finite; a program needn't handle non-finite values.
Results may differ from a plain program's by a relative error of at most 0.017.
Values may be sent and summed in bfloat16 or wider, within the bound.
A program may use at most 64 MiB of HBM per device.

v0:
```python
import jax
import jax.numpy as jnp
from jax import lax
from jax.sharding import PartitionSpec as P

epsilon = 1e-06


def normalize(row_data, norm_gain, norm_bias):
    values = row_data.astype(jnp.float32)
    row_mean = jnp.mean(values, axis=-1, keepdims=True)
    centred = values - row_mean
    inv_std = lax.rsqrt(jnp.mean(centred * centred, axis=-1, keepdims=True) + epsilon)
    standard = centred * inv_std
    normed = (standard * norm_gain + norm_bias).astype(jnp.bfloat16)
    return (standard, inv_std, normed)


def contract_tokens(left_rows, right_rows):
    return lax.dot_general(
        left_rows, right_rows, (((0,), (0,)), ((), ())), preferred_element_type=jnp.float32
    )


def body(first_out, second_out, grad_first, grad_second, w_up, w_down, norm_gain, norm_bias):
    own_rows = first_out.shape[0]
    up_full, down_full = (
        lax.all_gather(w_up, "dp", axis=0, tiled=True),
        lax.all_gather(w_down, "dp", axis=1, tiled=True),
    )
    first_all, grad_all = (
        lax.all_gather(first_out, "tensor", axis=0, tiled=True),
        lax.all_gather(grad_second, "tensor", axis=0, tiled=True),
    )
    standard_all, inv_std_all, normed = normalize(first_all, norm_gain, norm_bias)
    offset = lax.axis_index("tensor") * own_rows
    standard = lax.dynamic_slice_in_dim(standard_all, offset, own_rows, 0)
    inv_std = lax.dynamic_slice_in_dim(inv_std_all, offset, own_rows, 0)
    preact = jnp.dot(normed, up_full, preferred_element_type=jnp.float32)
    hidden = jax.nn.gelu(preact).astype(jnp.bfloat16)
    branch = lax.psum_scatter(
        jnp.dot(hidden, down_full, preferred_element_type=jnp.float32).astype(jnp.bfloat16),
        "tensor",
        scatter_dimension=0,
        tiled=True,
    ).astype(jnp.float32)
    second_in = (second_out.astype(jnp.float32) - branch).astype(jnp.bfloat16)
    tokens = own_rows * lax.axis_size("tensor") * lax.axis_size("dp")
    grad_scale = tokens ** (-0.5)
    grad_down_part = contract_tokens(hidden, grad_all)
    grad_down = (
        lax.psum_scatter(
            grad_down_part.astype(jnp.bfloat16), "dp", scatter_dimension=1, tiled=True
        ).astype(jnp.float32)
        * grad_scale
    )
    grad_hidden = lax.dot_general(
        grad_all, down_full, (((1,), (1,)), ((), ())), preferred_element_type=jnp.float32
    )
    grad_pre = jax.vjp(jax.nn.gelu, preact)[1](grad_hidden)[0].astype(jnp.bfloat16)
    grad_up_part = contract_tokens(normed, grad_pre)
    grad_up = (
        lax.psum_scatter(
            grad_up_part.astype(jnp.bfloat16), "dp", scatter_dimension=0, tiled=True
        ).astype(jnp.float32)
        * grad_scale
    )
    grad_normed = lax.psum_scatter(
        lax.dot_general(
            grad_pre, up_full, (((1,), (1,)), ((), ())), preferred_element_type=jnp.float32
        ).astype(jnp.bfloat16),
        "tensor",
        scatter_dimension=0,
        tiled=True,
    ).astype(jnp.float32)
    grad_std = grad_normed * norm_gain
    grad_rows = inv_std * (
        grad_std
        - jnp.mean(grad_std, axis=-1, keepdims=True)
        - standard * jnp.mean(grad_std * standard, axis=-1, keepdims=True)
    )
    grad_first_in = grad_first.astype(jnp.float32) + grad_rows
    local_stats = jnp.stack([jnp.sum(grad_normed * standard, axis=0), jnp.sum(grad_normed, axis=0)])
    grad_norm = lax.psum(local_stats, ("tensor", "dp")) * grad_scale
    return (second_in, grad_first_in, grad_up, grad_down, grad_norm)


def solution(mesh):
    in_specs = (
        P(("groups", "tensor", "dp"), None),
        P(("groups", "tensor", "dp"), None),
        P(("groups", "tensor", "dp"), None),
        P(("groups", "tensor", "dp"), None),
        P("dp", "tensor"),
        P("tensor", "dp"),
        P(),
        P(),
    )
    out_specs = (
        P(("groups", "tensor", "dp"), None),
        P(("groups", "tensor", "dp"), None),
        P(("groups", "dp"), "tensor"),
        P(("groups", "tensor"), "dp"),
        P("groups", None),
    )
    return jax.shard_map(body, mesh=mesh, in_specs=in_specs, out_specs=out_specs, check_vma=False)
```

profile of v0, /device:TPU:0, one launch (start us, length us, event | category | flops | bytes accessed | tf_op | source)
XLA Modules:
  0.0 442.5 jit_solution(17227224625132561028)
XLA Ops:
  7.2 0.0 all-gather.5.cloned.1.call-start
  7.2 0.7 all-gather.5.cloned.1.call-update
  7.9 0.0 all-gather.11.cloned.1.call-start
  7.9 0.7 all-gather.11.cloned.1.call-update
  8.7 0.0 all-gather.9.cloned.1.call-start
  8.7 0.7 all-gather.9.cloned.1.call-update
  9.4 0.0 all-gather.7.cloned.1.call-start
  9.4 0.5 all-gather.7.cloned.1.call-update
  10.0 0.0 reduce-scatter.7.cloned.1.call-start
  10.0 19.0 %all-gather.5.cloned.1.call-done = bf16[512,1024]{1,0:T(8,128)(2,1)} async-done(((bf16[128,1024]{1,0:T(8,128)(2,1)}), bf16[512,1024]{1,0:T(8,128)(2,1)}) %all-gather.5.cloned.1.call-update) | async-done | bytes 1048592 | tf_op jit(solution)/shard_map/all_gather | solution.py:32
  29.0 1.4 convert_reduce_fusion
  30.4 1.6 fusion.9
  32.1 0.0 copy-start
  32.1 0.0 copy-start.2
  32.1 0.0 copy-start.5
  32.1 15.2 %all-gather.11.cloned.1.call-done = bf16[512,1024]{1,0:T(8,128)(2,1)} async-done(((bf16[128,1024]{1,0:T(8,128)(2,1)}), bf16[512,1024]{1,0:T(8,128)(2,1)}) %all-gather.11.cloned.1.call-update) | async-done | bytes 1048592 | tf_op jit(solution)/shard_map/all_gather | solution.py:33
  47.3 82.1 %all-gather.9.cloned.1.call-done = bf16[2048,1024]{1,0:T(8,128)(2,1)} async-done(((bf16[2048,256]{1,0:T(8,128)(2,1)}), bf16[2048,1024]{1,0:T(8,128)(2,1)}) %all-gather.9.cloned.1.call-update) | async-done | bytes 4194320 | tf_op jit(solution)/shard_map/all_gather | solution.py:29
  129.4 6.9 %fusion.21 = f32[512,2048]{1,0:T(8,128)} fusion(bf16[512,1024]{1,0:T(8,128)(2,1)} %all-gather.11.cloned.1.call-done, bf16[2048,1024]{1,0:T(8,128)(2,1)} %all-gather.9.cloned.1.call-done), kind=kOutput, calls=%fused_computation.41 | convolution fusion | flops 2147483648 | bytes 9437184 | tf_op jit(solution)/shard_map/dot_general | solution.py:57
  136.3 73.5 %all-gather.7.cloned.1.call-done = bf16[1024,2048]{1,0:T(8,128)(2,1)} async-done(((bf16[256,2048]{1,0:T(8,128)(2,1)}), bf16[1024,2048]{1,0:T(8,128)(2,1)}) %all-gather.7.cloned.1.call-update) | async-done | bytes 4194320 | tf_op jit(solution)/shard_map/all_gather | solution.py:28
  209.8 0.0 copy-done
  209.8 0.0 copy-done.2
  209.8 0.0 copy-done.5
  209.8 0.0 copy-start.3
  209.8 9.5 %fusion.6 = (bf16[512,2048]{1,0:T(8,128)(2,1)S(1)}, f32[512,2048]{1,0:T(8,128)}) fusion(f32[512,2048]{1,0:T(8,128)} %fusion.21, bf16[1024,2048]{1,0:T(8,128)(2,1)} %all-gather.7.cloned.1.call-done, f32[1024]{0:T(1024)S(1)} %copy-done.5, f32[1024]{0:T(1024)S(1)} %copy-done.2, f32[512]{0:T(512)S(1)} %add_rsqrt_fusion, f32[512]{0:T(512)S(1)} %broadcast_multiply_fusion.1, ...), kind=kOutput, calls=%fused_computation.8 | convolution fusion | flops 2171600896 | bytes 15740928 | tf_op jit(solution)/shard_map/dot_general | solution.py:39
  219.3 0.0 copy-done.3
  219.3 3.4 convolution_convert_fusion.2
  222.7 0.0 reduce-scatter.7.cloned.1.call-update
  222.8 0.0 reduce-scatter.5.cloned.1.call-start
  222.8 7.1 %convolution_convert_fusion.3 = bf16[512,1024]{1,0:T(8,128)(2,1)} fusion(bf16[2048,1024]{1,0:T(8,128)(2,1)} %all-gather.9.cloned.1.call-done, f32[512,2048]{1,0:T(8,128)} %get-tuple-element.10), kind=kOutput, calls=%fused_computation.21 | convolution fusion | flops 2157445120 | bytes 9437184 | tf_op jit(solution)/shard_map/dot_general | solution.py:42
  229.9 0.0 reduce-scatter.5.cloned.1.call-update
  229.9 0.2 reduce-scatter.9.cloned.1.call-start
  230.2 4.6 %convolution_convert_fusion.1 = bf16[1024,2048]{1,0:T(8,128)(2,1)} fusion(bf16[512,2048]{1,0:T(8,128)(2,1)S(1)} %get-tuple-element.9, f32[1024]{0:T(1024)S(1)} %copy-done.5, f32[1024]{0:T(1024)S(1)} %copy-done.2, bf16[512,1024]{1,0:T(8,128)(2,1)S(1)} %copy-done, f32[512]{0:T(512)S(1)} %add_rsqrt_fusion, f32[512]{0:T(512)S(1)} %broadcast_multiply_fusion.1), kind=kOutput, calls=%fused_computation.11 | convolution fusion | flops 2152726528 | bytes 7352320 | tf_op jit(solution)/shard_map/dot_general | solution.py:20
  234.7 0.0 copy-start.4
  234.7 0.0 reduce-scatter.9.cloned.1.call-update
  234.7 0.0 reduce-scatter.11.cloned.1.call-start
  234.8 1.1 copy-done.4
  235.9 7.3 %convolution_convert_fusion = bf16[2048,1024]{1,0:T(8,128)(2,1)} fusion(bf16[512,1024]{1,0:T(8,128)(2,1)S(1)} %copy-done.4, f32[512,2048]{1,0:T(8,128)} %get-tuple-element.10), kind=kOutput, calls=%fused_computation.10 | convolution fusion | flops 2159017984 | bytes 9437184 | tf_op jit(solution)/shard_map/dot_general | solution.py:20
  243.2 0.0 copy-start.1
  243.2 0.0 reduce-scatter.11.cloned.1.call-update
  243.2 0.1 dynamic-slice.3
  243.3 0.3 fusion.7
  243.6 2.6 reduce-scatter.7.cloned.1.call-done
  246.2 1.2 fusion.17
  247.4 33.1 %psum.7 = f32[2,1024]{1,0:T(2,128)S(1)} all-reduce(f32[2,1024]{1,0:T(2,128)S(1)} %pad_maximum_fusion), channel_id=1, replica_groups=mesh['groups'=2,'tensor'=4,'dp'=4] {'tensor','dp'}, use_global_device_ids=true, to_apply=%region_10.0 | all-reduce | flops 2048 | bytes 16384 | tf_op jit(solution)/shard_map/psum | solution.py:84
  280.6 0.6 broadcast_multiply_fusion
  281.2 0.0 reduce-scatter.5.cloned.1.call-done
  281.2 0.0 copy-done.1
  281.2 1.7 subtract_convert_fusion
  282.9 2.1 fusion.15
  285.0 68.3 %reduce-scatter.9.cloned.1.call-done = bf16[256,2048]{1,0:T(8,128)(2,1)} async-done(((bf16[1024,2048]{1,0:T(8,128)(2,1)}), bf16[256,2048]{1,0:T(8,128)(2,1)}) %reduce-scatter.9.cloned.1.call-update) | async-done | bytes 1048592 | tf_op jit(solution)/shard_map/reduce_scatter | solution.py:63
  353.3 2.8 convert_multiply_fusion.1
  356.1 76.8 %reduce-scatter.11.cloned.1.call-done = bf16[2048,256]{1,0:T(8,128)(2,1)} async-done(((bf16[2048,1024]{1,0:T(8,128)(2,1)}), bf16[2048,256]{1,0:T(8,128)(2,1)}) %reduce-scatter.11.cloned.1.call-update) | async-done | bytes 1048592 | tf_op jit(solution)/shard_map/reduce_scatter | solution.py:52
  432.9 2.7 convert_multiply_fusion
  (4 shorter events, 0.0 us)
Async XLA Ops:
  7.2 21.8 %all-gather.5.cloned.1.call-start = ((), (), s32[]{:S(2)}) async-start(), calls=%async_computation.4 | async-start | bytes 1310720 | tf_op jit(solution)/shard_map/all_gather | solution.py:32
  7.9 39.4 %all-gather.11.cloned.1.call-start = ((), (), s32[]{:S(2)}) async-start(), calls=%async_computation.8 | async-start | bytes 1310720 | tf_op jit(solution)/shard_map/all_gather | solution.py:33
  8.7 120.8 %all-gather.9.cloned.1.call-start = ((), (), s32[]{:S(2)}) async-start(), calls=%async_computation.6 | async-start | bytes 5242880 | tf_op jit(solution)/shard_map/all_gather | solution.py:29
  9.4 200.4 %all-gather.7.cloned.1.call-start = ((), (), s32[]{:S(2)}) async-start(), calls=%async_computation.5 | async-start | bytes 5242880 | tf_op jit(solution)/shard_map/all_gather | solution.py:28
  10.0 236.3 %reduce-scatter.7.cloned.1.call-start = ((), (), s32[]{:S(2)}) async-start(), calls=%async_computation.9 | async-start | bytes 1310720 | tf_op jit(solution)/shard_map/reduce_scatter | solution.py:68
  32.1 177.7 %copy-start = (bf16[512,1024]{1,0:T(8,128)(2,1)S(1)}, bf16[512,1024]{1,0:T(8,128)(2,1)}, u32[]{:S(2)}) copy-start(bf16[512,1024]{1,0:T(8,128)(2,1)} %all-gather.5.cloned.1.call-done) | copy-start | bytes 3145732
  32.1 177.7 %copy-start.2 = (f32[1024]{0:T(1024)S(1)}, f32[1024]{0:T(1024)}, u32[]{:S(2)}) copy-start(f32[1024]{0:T(1024)} %param.14) | copy-start | bytes 12292
  32.1 177.7 %copy-start.5 = (f32[1024]{0:T(1024)S(1)}, f32[1024]{0:T(1024)}, u32[]{:S(2)}) copy-start(f32[1024]{0:T(1024)} %param.15) | copy-start | bytes 12292
  209.8 9.5 %copy-start.3 = (bf16[1024,2048]{1,0:T(8,128)(2,1)S(1)}, bf16[1024,2048]{1,0:T(8,128)(2,1)}, u32[]{:S(2)}) copy-start(bf16[1024,2048]{1,0:T(8,128)(2,1)} %all-gather.7.cloned.1.call-done) | copy-start | bytes 12582916
  222.8 58.4 %reduce-scatter.5.cloned.1.call-start = ((), (), s32[]{:S(2)}) async-start(), calls=%async_computation.7 | async-start | bytes 1310720 | tf_op jit(solution)/shard_map/reduce_scatter | solution.py:41
  229.9 123.3 %reduce-scatter.9.cloned.1.call-start = ((), (), s32[]{:S(2)}) async-start(), calls=%async_computation.10 | async-start | bytes 5242880 | tf_op jit(solution)/shard_map/reduce_scatter | solution.py:63
  234.7 1.2 copy-start.4
  234.7 198.1 %reduce-scatter.11.cloned.1.call-start = ((), (), s32[]{:S(2)}) async-start(), calls=%async_computation.11 | async-start | bytes 5242880 | tf_op jit(solution)/shard_map/reduce_scatter | solution.py:52
  243.2 38.0 %copy-start.1 = (bf16[128,1024]{1,0:T(8,128)(2,1)S(1)}, bf16[128,1024]{1,0:T(8,128)(2,1)}, u32[]{:S(2)}) copy-start(bf16[128,1024]{1,0:T(8,128)(2,1)} %param.9) | copy-start | bytes 786436
Sparse Core Ops, SparseCore 0:
  9.5 19.4 all-gather.4
  30.6 16.6 all-gather.10
  48.9 80.5 all-gather.8
  130.8 78.9 all-gather.6
  222.9 23.2 reduce-scatter.6
  249.2 24.8 reduce-scatter.4
  276.3 76.8 reduce-scatter.8
  355.5 77.2 reduce-scatter.10
where the time goes:
time: 443 us; the launch traced here: 442 us
  waiting for transfers between devices  340 us (77%)
  matrix products  38.7 us (9%)
  blocking collectives  33.1 us (7%)
  other arithmetic  14.5 us (3%)
  between operations  14.2 us (3%)
    all_gather x1, waiting for transfers between devices, body(): lax.all_gather(w_down, 'dp', axis=1, tiled=True)  82.1 us
    reduce_scatter x1, waiting for transfers between devices, body(): lax.psum_scatter(grad_down_part.astype(jnp.bfloat16), 'dp', scatter_dimen...  76.8 us
    all_gather x1, waiting for transfers between devices, body(): lax.all_gather(w_up, 'dp', axis=0, tiled=True)  73.5 us
    reduce_scatter x1, waiting for transfers between devices, body(): lax.psum_scatter(grad_up_part.astype(jnp.bfloat16), 'dp', scatter_dimensi...  68.3 us
    psum x1, blocking collectives, body(): grad_norm = lax.psum(local_stats, ('tensor', 'dp')) * grad_scale  33.1 us
    all_gather x1, waiting for transfers between devices, body(): lax.all_gather(first_out, 'tensor', axis=0, tiled=True)  19 us
    all_gather x1, waiting for transfers between devices, body(): lax.all_gather(grad_second, 'tensor', axis=0, tiled=True)  15.2 us
    dot_general x2, matrix products, contract_tokens(): lax.dot_general(left_rows, right_rows, (((0,), (0,)), ((), ())), preferre...  11.8 us
  transfers between devices with their start and end apart: 8, of which 7 were waited for; matrix products, arithmetic and copies ran while one was open for 8% of the time, Pallas kernels for 0%

commit v1 on v0

--- a/solution.py
+++ b/solution.py
@@ -1,6 +1,10 @@
+import functools
+
 import jax
 import jax.numpy as jnp
 from jax import lax
+from jax.experimental import pallas as pl
+from jax.experimental.pallas import tpu as pltpu
 from jax.sharding import PartitionSpec as P
 
 epsilon = 1e-06
@@ -85,6 +89,548 @@
     return (second_in, grad_first_in, grad_up, grad_down, grad_norm)
 
 
+def span(index, size):
+    return pl.ds(pl.multiple_of(index * size, size), size)
+
+
+def flipped(index, mask, bits):
+    for bit in range(bits):
+        if mask >> bit & 1:
+            step = 1 << bit
+            index = index + (1 - 2 * ((index // step) % 2)) * step
+    return index
+
+
+def greet(n_groups, n_dp, bits, group, tensor, dp):
+    barrier = pltpu.get_barrier_semaphore()
+    peers = [{"dp": (dp + s) % n_dp} for s in range(1, n_dp)]
+    peers += [{"tensor": flipped(tensor, 1 << bit, bits)} for bit in range(bits)]
+    peers += [{"groups": (group + s) % n_groups} for s in range(1, n_groups)]
+    for peer in peers:
+        pl.semaphore_signal(
+            barrier, inc=1, device_id=peer, device_id_type=pl.DeviceIdType.MESH
+        )
+    pl.semaphore_wait(barrier, len(peers))
+
+
+def remote(src, dst, sems, index, peer):
+    return pltpu.make_async_remote_copy(
+        src_ref=src,
+        dst_ref=dst,
+        send_sem=sems[0].at[index],
+        recv_sem=sems[1].at[index],
+        device_id=peer,
+        device_id_type=pl.DeviceIdType.MESH,
+    )
+
+
+def gather_kernel(
+    n_groups, n_tensor, n_dp,
+    normed_ref, grad_ref, w_up_ref, w_down_ref,
+    normed_all, grad_all, up_ref, down_ref,
+    local_sem, line_send, line_recv, column_send, column_recv,
+    weight_send, weight_recv, share_send, share_recv,
+):
+    group, tensor, dp = (lax.axis_index(name) for name in ("groups", "tensor", "dp"))
+    bits = n_tensor.bit_length() - 1
+    rows = normed_ref.shape[0]
+    depth = w_up_ref.shape[0]
+    units = w_up_ref.shape[1] // n_dp
+    inputs, outputs = (normed_ref, grad_ref), (normed_all, grad_all)
+    line_sems, column_sems = (line_send, line_recv), (column_send, column_recv)
+    weight_sems, share_sems = (weight_send, weight_recv), (share_send, share_recv)
+
+    def block(a, mask, source):
+        return outputs[a].at[span(flipped(tensor, mask, bits) * n_dp + source, rows), :]
+
+    def place(k):
+        if k == 0:
+            return dp, None
+        if k < n_dp:
+            return dp - k, dp >= k
+        return dp + (k - n_dp + 1), dp + (k - n_dp + 1) <= n_dp - 1
+
+    def guarded(conditions, action):
+        conditions = [c for c in conditions if c is not None]
+        if not conditions:
+            action()
+        else:
+            pl.when(functools.reduce(jnp.logical_and, conditions))(action)
+
+    def line_copy(a, side, distance):
+        if side == 0:
+            source, target = dp - (distance - 1), dp + 1
+        else:
+            source, target = dp + (distance - 1), dp - 1
+        src = inputs[a] if distance == 1 else block(a, 0, source)
+        return remote(src, block(a, 0, source), line_sems, (a, side, distance), {"dp": target})
+
+    def line_send_conditions(side, distance):
+        if side == 0:
+            return [dp >= distance - 1 if distance > 1 else None, dp <= n_dp - 2]
+        return [dp <= n_dp - distance if distance > 1 else None, dp >= 1]
+
+    def column_copy(a, mask, k, bit):
+        source, _ = place(k)
+        src = inputs[a] if mask == 0 and k == 0 else block(a, mask, source)
+        return remote(
+            src, block(a, mask, source), column_sems, (a, mask | 1 << bit, k),
+            {"tensor": flipped(tensor, 1 << bit, bits)},
+        )
+
+    def column_arrival(a, mask, k):
+        source, _ = place(k)
+        bit = (mask & -mask).bit_length() - 1
+        here = block(a, mask, source)
+        return remote(
+            here, here, column_sems, (a, mask, k), {"tensor": flipped(tensor, 1 << bit, bits)}
+        )
+
+    def next_bits(mask):
+        top = bits if mask == 0 else (mask & -mask).bit_length() - 1
+        return list(reversed(range(top)))
+
+    def pass_on(a, mask, k):
+        for bit in next_bits(mask):
+            column_copy(a, mask, k, bit).start()
+
+    part = depth // n_groups
+    piece = units // n_groups
+
+    def weight_views(kind, source, owner):
+        if kind == 0:
+            return up_ref.at[span(source * n_groups + owner, part), :]
+        return down_ref.at[span(owner, piece), span(source, depth)]
+
+    def weight_copy(kind, s):
+        target = (dp + s) % n_dp
+        if kind == 0:
+            src = w_up_ref.at[span(group, part), span(target, units)]
+        else:
+            src = w_down_ref.at[span(target * n_groups + group, piece), :]
+        return remote(src, weight_views(kind, dp, group), weight_sems, (kind, s), {"dp": target})
+
+    def weight_arrival(kind, s):
+        here = weight_views(kind, (dp + n_dp - s) % n_dp, group)
+        return remote(here, here, weight_sems, (kind, s), {"dp": (dp + s) % n_dp})
+
+    def share_copy(kind, s, h):
+        here = weight_views(kind, (dp + n_dp - s) % n_dp, group)
+        return remote(here, here, share_sems, (kind, s, h), {"groups": (group + h) % n_groups})
+
+    def share_arrival(kind, s, h):
+        here = weight_views(kind, (dp + n_dp - s) % n_dp, (group + n_groups - h) % n_groups)
+        return remote(here, here, share_sems, (kind, s, h), {"groups": (group + h) % n_groups})
+
+    greet(n_groups, n_dp, bits, group, tensor, dp)
+    order = [0] + [k for s in range(1, n_dp) for k in (s, s + n_dp - 1)]
+    for a in range(2):
+        for side in range(2):
+            guarded(line_send_conditions(side, 1), lambda a=a, side=side: line_copy(a, side, 1).start())
+        pass_on(a, 0, 0)
+    for s in range(1, n_dp):
+        for kind in range(2):
+            weight_copy(kind, s).start()
+    local = [
+        pltpu.make_async_copy(inputs[a], block(a, 0, dp), local_sem.at[a]) for a in range(2)
+    ]
+    local.append(
+        pltpu.make_async_copy(
+            w_up_ref.at[:, span(dp, units)], up_ref.at[span(dp, depth), :], local_sem.at[2]
+        )
+    )
+    local.append(
+        pltpu.make_async_copy(
+            w_down_ref.at[span(dp, units), :], down_ref.at[:, span(dp, depth)], local_sem.at[3]
+        )
+    )
+    for copy in local:
+        copy.start()
+
+    through = [m for m in range(1, n_tensor) if next_bits(m)]
+    final = [m for m in range(1, n_tensor) if not next_bits(m)]
+
+    def relay(k):
+        for a in range(2):
+            for mask in sorted(through, reverse=True):
+                def action(a=a, mask=mask):
+                    column_arrival(a, mask, k).wait_recv()
+                    pass_on(a, mask, k)
+                guarded([place(k)[1]], action)
+
+    done = [[0]] + [[s, s + n_dp - 1] for s in range(1, n_dp)]
+    for s in range(1, n_dp):
+        for a in range(2):
+            for side in range(2):
+                k = done[s][side]
+
+                def action(a=a, side=side, k=k, s=s):
+                    source, _ = place(k)
+                    here = block(a, 0, source)
+                    remote(here, here, line_sems, (a, side, s), {"dp": (dp + 1) % n_dp}).wait_recv()
+                    if s < n_dp - 1:
+                        guarded(
+                            line_send_conditions(side, s + 1),
+                            lambda: line_copy(a, side, s + 1).start(),
+                        )
+                    pass_on(a, 0, k)
+
+                guarded([place(k)[1]], action)
+        for k in done[s - 1]:
+            relay(k)
+        for kind in range(2):
+            weight_arrival(kind, s).wait_recv()
+            for h in range(1, n_groups):
+                share_copy(kind, s, h).start()
+    for k in done[n_dp - 1]:
+        relay(k)
+    for k in order:
+        for a in range(2):
+            for mask in final:
+                guarded([place(k)[1]], lambda a=a, mask=mask, k=k: column_arrival(a, mask, k).wait_recv())
+    for s in range(1, n_dp):
+        for kind in range(2):
+            weight_copy(kind, s).wait_send()
+            for h in range(1, n_groups):
+                share_arrival(kind, s, h).wait_recv()
+                share_copy(kind, s, h).wait_send()
+    for a in range(2):
+        for side in range(2):
+            for s in range(1, n_dp):
+                guarded(
+                    line_send_conditions(side, s),
+                    lambda a=a, side=side, s=s: line_copy(a, side, s).wait_send(),
+                )
+        for mask in [0] + through:
+            for k in order:
+                for bit in next_bits(mask):
+                    guarded(
+                        [place(k)[1]],
+                        lambda a=a, mask=mask, k=k, bit=bit: column_copy(a, mask, k, bit).wait_send(),
+                    )
+    for copy in local:
+        copy.wait()
+
+
+def scatter_kernel(
+    n_groups, n_tensor, n_dp, grad_scale,
+    branch_ref, back_ref, g_up_ref, g_down_ref, first_ref, second_ref, grad_ref, gain_ref,
+    second_in_ref, grad_first_ref, grad_norm_ref, up_out, down_out,
+    fold, right, left, stat_line, stat_fold, local_sem,
+    fold_send, fold_recv, line_send, line_recv, grads_send, grads_recv,
+    stat_send, stat_recv, pair_send, pair_recv,
+):
+    group, tensor, dp = (lax.axis_index(name) for name in ("groups", "tensor", "dp"))
+    bits = n_tensor.bit_length() - 1
+    rows, width = first_ref.shape
+    units = g_up_ref.shape[1]
+    depth = g_up_ref.shape[0] // n_dp
+    partials = (branch_ref, back_ref)
+    fold_sems, line_sems = (fold_send, fold_recv), (line_send, line_recv)
+    grads_sems, stat_sems, pair_sems = (
+        (grads_send, grads_recv), (stat_send, stat_recv), (pair_send, pair_recv),
+    )
+    slots = {}
+    for bit in range(bits):
+        for mask in range(0, n_tensor, 2 << bit):
+            slots[bit, mask] = len(slots)
+
+    def grads_copy(kind, s):
+        target = (dp + s) % n_dp
+        if kind == 0:
+            src, dst = g_up_ref.at[span(target, depth), :], up_out.at[:, span(dp, units)]
+        else:
+            src, dst = g_down_ref.at[:, span(target, depth)], down_out.at[span(dp, units), :]
+        return remote(src, dst, grads_sems, (kind, s), {"dp": target})
+
+    def grads_arrival(kind, s):
+        source = (dp + n_dp - s) % n_dp
+        here = up_out.at[:, span(source, units)] if kind == 0 else down_out.at[span(source, units), :]
+        return remote(here, here, grads_sems, (kind, s), {"dp": (dp + s) % n_dp})
+
+    def current(a, bit, mask, b):
+        if bit == 0:
+            return partials[a].at[span(flipped(tensor, mask, bits) * n_dp + b, rows), :]
+        return fold.at[a, slots[bit - 1, mask], b]
+
+    def fold_copy(a, bit, mask, b):
+        slot = slots[bit, mask ^ 1 << bit]
+        return remote(
+            current(a, bit, mask, b), fold.at[a, slot, b], fold_sems, (a, slot, b),
+            {"tensor": flipped(tensor, 1 << bit, bits)},
+        )
+
+    def fold_arrival(a, bit, mask, b):
+        slot = slots[bit, mask]
+        here = fold.at[a, slot, b]
+        return remote(
+            here, here, fold_sems, (a, slot, b), {"tensor": flipped(tensor, 1 << bit, bits)}
+        )
+
+    def add_into(ref, other):
+        @pl.loop(0, rows // 16)
+        def _(i):
+            cut = pl.ds(pl.multiple_of(i * 16, 16), 16)
+            ref[cut, :] = (
+                ref[cut, :].astype(jnp.float32) + other[cut, :].astype(jnp.float32)
+            ).astype(ref.dtype)
+
+    greet(n_groups, n_dp, bits, group, tensor, dp)
+
+    def sent_masks(bit):
+        masks = [m for m in range(n_tensor) if m % (1 << bit) == 0 and m >> bit & 1]
+        return sorted(masks, reverse=True)
+
+    def kept_masks(bit):
+        return sorted(range(0, n_tensor, 2 << bit), reverse=True)
+
+    for mask in sent_masks(0):
+        for b in range(n_dp):
+            for a in range(2):
+                fold_copy(a, 0, mask, b).start()
+    for s in range(1, n_dp):
+        for kind in range(2):
+            grads_copy(kind, s).start()
+    local = [
+        pltpu.make_async_copy(
+            g_up_ref.at[span(dp, depth), :], up_out.at[:, span(dp, units)], local_sem.at[0]
+        ),
+        pltpu.make_async_copy(
+            g_down_ref.at[:, span(dp, depth)], down_out.at[span(dp, units), :], local_sem.at[1]
+        ),
+    ]
+    for copy in local:
+        copy.start()
+    for bit in range(bits):
+        for mask in kept_masks(bit):
+            for b in range(n_dp):
+                for a in range(2):
+                    fold_arrival(a, bit, mask, b).wait_recv()
+                    add_into(fold.at[a, slots[bit, mask], b], current(a, bit, mask, b))
+                    if bit + 1 < bits and mask in sent_masks(bit + 1):
+                        fold_copy(a, bit + 1, mask, b).start()
+
+    last = slots[bits - 1, 0]
+    moving = (right, left)
+
+    def line_conditions(side, s):
+        return dp + s <= n_dp - 1 if side == 0 else dp >= s
+
+    def behind(side):
+        return dp >= 1 if side == 0 else dp <= n_dp - 2
+
+    def line_peer(side):
+        return {"dp": (dp + 1) % n_dp if side == 0 else (dp + n_dp - 1) % n_dp}
+
+    def line_copy(a, side, s, relayed):
+        target = dp + s if side == 0 else dp - s
+        src = moving[side].at[a, s] if relayed else fold.at[a, last, target]
+        return remote(src, moving[side].at[a, s - 1], line_sems, (a, side, s - 1), line_peer(side))
+
+    def line_arrival(a, side, s):
+        here = moving[side].at[a, s]
+        return remote(here, here, line_sems, (a, side, s), line_peer(side))
+
+    for s in range(n_dp - 1, 0, -1):
+        for a in range(2):
+            for side in range(2):
+                @pl.when(jnp.logical_and(line_conditions(side, s), jnp.logical_not(behind(side))))
+                def _(a=a, side=side, s=s):
+                    line_copy(a, side, s, False).start()
+
+                if s <= n_dp - 2:
+                    @pl.when(jnp.logical_and(line_conditions(side, s), behind(side)))
+                    def _(a=a, side=side, s=s):
+                        target = dp + s if side == 0 else dp - s
+                        line_arrival(a, side, s).wait_recv()
+                        add_into(moving[side].at[a, s], fold.at[a, last, target])
+                        line_copy(a, side, s, True).start()
+
+    for a in range(2):
+        for side in range(2):
+            @pl.when(behind(side))
+            def _(a=a, side=side):
+                line_arrival(a, side, 0).wait_recv()
+
+            @pl.when(jnp.logical_not(behind(side)))
+            def _(a=a, side=side):
+                moving[side][a, 0] = jnp.zeros((rows, width), moving[side].dtype)
+
+    stat_line[dp] = jnp.zeros(stat_line.shape[1:], jnp.float32)
+
+    @pl.loop(0, rows // 16)
+    def _(i):
+        cut = pl.ds(pl.multiple_of(i * 16, 16), 16)
+
+        def total(a):
+            return (
+                fold[a, last, dp, cut, :].astype(jnp.float32)
+                + right[a, 0, cut, :].astype(jnp.float32)
+                + left[a, 0, cut, :].astype(jnp.float32)
+            )
+
+        second_in_ref[cut, :] = (second_ref[cut, :].astype(jnp.float32) - total(0)).astype(
+            second_in_ref.dtype
+        )
+        standard, inv_std = standardize(first_ref[cut, :])
+        grad_normed = total(1)
+        stat_line[dp, 0:1, :] += jnp.sum(grad_normed * standard, axis=0, keepdims=True)
+        stat_line[dp, 1:2, :] += jnp.sum(grad_normed, axis=0, keepdims=True)
+        grad_std = grad_normed * gain_ref[...]
+        grad_rows = inv_std * (
+            grad_std
+            - jnp.mean(grad_std, axis=-1, keepdims=True)
+            - standard * jnp.mean(grad_std * standard, axis=-1, keepdims=True)
+        )
+        grad_first_ref[cut, :] = grad_ref[cut, :].astype(jnp.float32) + grad_rows
+
+    def stat_copy(s):
+        here = stat_line.at[dp]
+        return remote(here, here, stat_sems, s, {"dp": (dp + s) % n_dp})
+
+    def stat_arrival(s):
+        here = stat_line.at[(dp + n_dp - s) % n_dp]
+        return remote(here, here, stat_sems, s, {"dp": (dp + s) % n_dp})
+
+    for s in range(1, n_dp):
+        stat_copy(s).start()
+    for s in range(1, n_dp):
+        stat_arrival(s).wait_recv()
+    sums = stat_line[0]
+    for source in range(1, n_dp):
+        sums = sums + stat_line[source]
+    for bit in range(bits):
+        stat_fold[bit, 0] = sums
+        copy = remote(
+            stat_fold.at[bit, 0], stat_fold.at[bit, 1], pair_sems, bit,
+            {"tensor": flipped(tensor, 1 << bit, bits)},
+        )
+        copy.start()
+        copy.wait()
+        sums = stat_fold[bit, 0] + stat_fold[bit, 1]
+    grad_norm_ref[...] = sums[0:2] * grad_scale
+
+    for s in range(1, n_dp):
+        stat_copy(s).wait_send()
+        for kind in range(2):
+            grads_arrival(kind, s).wait_recv()
+            grads_copy(kind, s).wait_send()
+    for copy in local:
+        copy.wait()
+    for bit in range(bits):
+        for mask in sent_masks(bit):
+            for b in range(n_dp):
+                for a in range(2):
+                    fold_copy(a, bit, mask, b).wait_send()
+    for s in range(n_dp - 1, 0, -1):
+        for a in range(2):
+            for side in range(2):
+                @pl.when(line_conditions(side, s))
+                def _(a=a, side=side, s=s):
+                    line_copy(a, side, s, s <= n_dp - 2).wait_send()
+
+
+def standardize(row_data):
+    values = row_data.astype(jnp.float32)
+    centred = values - jnp.mean(values, axis=-1, keepdims=True)
+    inv_std = lax.rsqrt(jnp.mean(centred * centred, axis=-1, keepdims=True) + epsilon)
+    return centred * inv_std, inv_std
+
+
+ANY = pl.BlockSpec(memory_space=pl.ANY)
+VMEM = pl.BlockSpec(memory_space=pltpu.VMEM)
+DMA = pltpu.SemaphoreType.DMA
+
+
+def spread_body(sizes, first_out, second_out, grad_first, grad_second, w_up, w_down, norm_gain, norm_bias):
+    n_groups, n_tensor, n_dp = sizes
+    rows, width = first_out.shape
+    tokens = rows * n_tensor * n_dp
+    units = w_up.shape[1] // n_dp
+    bits = n_tensor.bit_length() - 1
+    half = jnp.bfloat16
+    grad_scale = tokens ** (-0.5)
+    _, _, own_normed = normalize(first_out, norm_gain, norm_bias)
+    normed, grad_all, up, down = pl.pallas_call(
+        functools.partial(gather_kernel, n_groups, n_tensor, n_dp),
+        out_shape=(
+            jax.ShapeDtypeStruct((tokens, width), half),
+            jax.ShapeDtypeStruct((tokens, width), half),
+            jax.ShapeDtypeStruct((width, units), half),
+            jax.ShapeDtypeStruct((units, width), half),
+        ),
+        in_specs=[VMEM] * 4,
+        out_specs=(ANY,) * 4,
+        scratch_shapes=[DMA((4,))]
+        + [DMA((2, 2, n_dp))] * 2
+        + [DMA((2, n_tensor, 2 * n_dp - 1))] * 2
+        + [DMA((2, n_dp))] * 2
+        + [DMA((2, n_dp, n_groups))] * 2,
+        compiler_params=pltpu.CompilerParams(collective_id=0, has_side_effects=True),
+        name="gather_all",
+    )(own_normed, grad_second, w_up, w_down)
+
+    preact = jnp.dot(normed, up, preferred_element_type=jnp.float32)
+    hidden = jax.nn.gelu(preact).astype(half)
+    grad_hidden = lax.dot_general(
+        grad_all, down, (((1,), (1,)), ((), ())), preferred_element_type=jnp.float32
+    )
+    grad_pre = jax.vjp(jax.nn.gelu, preact)[1](grad_hidden)[0].astype(half)
+    branch = jnp.dot(hidden, down, preferred_element_type=jnp.float32).astype(half)
+    back = lax.dot_general(
+        grad_pre, up, (((1,), (1,)), ((), ())), preferred_element_type=jnp.float32
+    ).astype(half)
+    g_down = contract_tokens(hidden, grad_all).astype(half)
+    g_up = contract_tokens(normed, grad_pre).astype(half)
+
+    second_in, grad_first_in, grad_norm, up_out, down_out = pl.pallas_call(
+        functools.partial(scatter_kernel, n_groups, n_tensor, n_dp, grad_scale),
+        out_shape=(
+            jax.ShapeDtypeStruct((rows, width), half),
+            jax.ShapeDtypeStruct((rows, width), jnp.float32),
+            jax.ShapeDtypeStruct((2, width), jnp.float32),
+            jax.ShapeDtypeStruct((w_up.shape[0], w_up.shape[1]), half),
+            jax.ShapeDtypeStruct((w_down.shape[0], w_down.shape[1]), half),
+        ),
+        in_specs=[VMEM] * 8,
+        out_specs=(VMEM,) * 3 + (ANY,) * 2,
+        scratch_shapes=[
+            pltpu.VMEM((2, n_tensor - 1, n_dp, rows, width), half),
+            pltpu.VMEM((2, n_dp - 1, rows, width), half),
+            pltpu.VMEM((2, n_dp - 1, rows, width), half),
+            pltpu.VMEM((n_dp, 8, width), jnp.float32),
+            pltpu.VMEM((bits, 2, 8, width), jnp.float32),
+            DMA((2,)),
+        ]
+        + [DMA((2, n_tensor - 1, n_dp))] * 2
+        + [DMA((2, 2, n_dp - 1))] * 2
+        + [DMA((2, n_dp))] * 2
+        + [DMA((n_dp,))] * 2
+        + [DMA((bits,))] * 2,
+        compiler_params=pltpu.CompilerParams(collective_id=1, has_side_effects=True),
+        name="scatter_all",
+    )(branch, back, g_up, g_down, first_out, second_out, grad_first, norm_gain.reshape(1, -1))
+    grad_up = up_out.astype(jnp.float32) * grad_scale
+    grad_down = down_out.astype(jnp.float32) * grad_scale
+    return second_in, grad_first_in, grad_up, grad_down, grad_norm
+
+
+def choose(sizes, *args):
+    first_out, w_up = args[0], args[4]
+    n_groups, n_tensor, n_dp = sizes
+    tokens = first_out.shape[0] * n_tensor * n_dp
+    fits = (
+        n_tensor > 1
+        and n_dp > 1
+        and n_tensor & (n_tensor - 1) == 0
+        and w_up.shape[1] % (n_dp * n_groups * 128) == 0
+        and w_up.shape[0] % (n_groups * 128) == 0
+    )
+    if fits and tokens <= w_up.shape[1]:
+        return spread_body(sizes, *args)
+    return body(*args)
+
+
 def solution(mesh):
     in_specs = (
         P(("groups", "tensor", "dp"), None),
@@ -103,4 +649,5 @@
         P(("groups", "tensor"), "dp"),
         P("groups", None),
     )
-    return jax.shard_map(body, mesh=mesh, in_specs=in_specs, out_specs=out_specs, check_vma=False)
+    sizes = tuple(mesh.shape[name] for name in ("groups", "tensor", "dp"))
+    return jax.shard_map(functools.partial(choose, sizes), mesh=mesh, in_specs=in_specs, out_specs=out_specs, check_vma=False)

time: 443 us -> 211 us (0.48)
  waiting for transfers between devices: 340 us -> 0 us
  Pallas kernels: 0 us -> 172 us
  blocking collectives: 33.1 us -> 0 us
  between operations: 14.2 us -> 0.74 us
  matrix products: 38.7 us -> 26.8 us
  other arithmetic: 14.5 us -> 9.77 us
    all_gather x4 -> x0, waiting for transfers between devices: 190 us -> none  [the longest x1 82.1 us: body(): lax.all_gather(w_down, 'dp', axis=1, tiled=True)]
    pallas_call x0 -> x2, Pallas kernels: none -> 172 us  [the longest x1 103 us: spread_body(): pl.pallas_call(functools.partial(scatter_kernel, n_groups, n_tensor, n_dp...]
    reduce_scatter x4 -> x0, waiting for transfers between devices: 148 us -> none  [the longest x1 76.8 us: body(): lax.psum_scatter(grad_down_part.astype(jnp.bfloat16), 'dp', scatter_dimen...]
    psum x1 -> x0, blocking collectives: 33.1 us -> none  [body(): grad_norm = lax.psum(local_stats, ('tensor', 'dp')) * grad_scale]
    dot_general x4, matrix products: 26.9 us -> 20 us  [the longest x1 5.96 us: spread_body(): preact = jnp.dot(normed, up, preferred_element_type=jnp.float32)]
    dot_general x2, matrix products: 11.8 us -> 6.78 us  [contract_tokens(): lax.dot_general(left_rows, right_rows, (((0,), (0,)), ((), ())), preferre...]
  transfers between devices with their start and end apart: 8 -> 0, of which waited for: 7 -> 0; matrix products, arithmetic and copies ran while one was open for 8% -> 0% of each run, Pallas kernels for 0% -> 0%
where the time goes in v1:
time: 211 us
  Pallas kernels  172 us (82%)
  matrix products  26.8 us (13%)
  other arithmetic  9.77 us (5%)
  local copies, waits for them, and re-layouts  2.12 us (1%)
    pallas_call x1, Pallas kernels, spread_body(): pl.pallas_call(functools.partial(scatter_kernel, n_groups, n_tensor, n_dp...  103 us
    pallas_call x1, Pallas kernels, spread_body(): pl.pallas_call(functools.partial(gather_kernel, n_groups, n_tensor, n_dp)...  69.2 us
    dot_general x2, matrix products, contract_tokens(): lax.dot_general(left_rows, right_rows, (((0,), (0,)), ((), ())), preferre...  6.78 us
    dot_general x1, matrix products, spread_body(): preact = jnp.dot(normed, up, preferred_element_type=jnp.float32)  5.96 us
    dot_general x1, matrix products, spread_body(): lax.dot_general(grad_all, down, (((1,), (1,)), ((), ())), preferred_eleme...  5.02 us
    dot_general x1, matrix products, spread_body(): jnp.dot(hidden, down, preferred_element_type=jnp.float32).astype(half)  4.76 us
    dot_general x1, matrix products, spread_body(): lax.dot_general(grad_pre, up, (((1,), (1,)), ((), ())), preferred_element...  4.31 us

profile of v1, /device:TPU:0, one launch (start us, length us, event | category | flops | bytes accessed | tf_op | source)
XLA Modules:
  0.0 211.2 jit_solution(6488275076813030354)
XLA Ops:
  0.6 1.1 convert_reduce_fusion
  1.7 1.2 fusion.9
  2.9 1.9 fusion.12.normed_ref
  4.8 69.2 %gather_all.1 = (bf16[2048,1024]{1,0:T(8,128)(2,1)}, bf16[2048,1024]{1,0:T(8,128)(2,1)}, bf16[1024,512]{1,0:T(8,128)(2,1)}, bf16[512,1024]{1,0:T(8,128)(2,1)}) custom-call(bf16[128,1024]{1,0:T(8,128)(2,1)} %fusion.12.normed_ref, bf16[128,1024]{1,0:T(8,128)(2,1)} %grad_ref.2, bf16[256,2048]{1,0:T(8,128)(2,1)} %w_up_ref.1, bf16[2048,256]{1,0:T(8,128)(2,1)} %w_down_ref.1), custom_call_target="tpu_custom_call" | custom-call | tf_op jit(solution)/shard_map/gather_all/pallas_call | solution.py:554
  74.0 0.0 copy-start.3
  74.0 0.0 copy-start.6
  74.0 5.0 %fusion.13 = f32[2048,512]{1,0:T(8,128)S(1)} fusion(bf16[2048,1024]{1,0:T(8,128)(2,1)} %get-tuple-element.17, bf16[512,1024]{1,0:T(8,128)(2,1)} %get-tuple-element.16), kind=kOutput, calls=%fused_computation.26 | convolution fusion | flops 2147483648 | bytes 9437184 | tf_op jit(solution)/shard_map/dot_general | solution.py:575
  79.1 0.0 copy-done.3
  79.1 0.0 copy-done.6
  79.1 0.0 copy-start.4
  79.1 6.0 %fusion.6 = (bf16[2048,512]{1,0:T(8,128)(2,1)S(1)}, f32[2048,512]{1,0:T(8,128)S(1)}) fusion(f32[2048,512]{1,0:T(8,128)S(1)} %fusion.13, bf16[2048,1024]{1,0:T(8,128)(2,1)S(1)} %copy-done.3, bf16[1024,512]{1,0:T(8,128)(2,1)S(1)} %copy-done.6), kind=kOutput, calls=%fused_computation.8 | convolution fusion | flops 2168455168 | bytes 15728640 | tf_op jit(solution)/shard_map/dot_general | solution.py:573
  85.1 0.0 copy-done.4
  85.1 3.4 %convolution_convert_fusion.2.g_down_ref = bf16[512,1024]{1,0:T(8,128)(2,1)} fusion(bf16[2048,1024]{1,0:T(8,128)(2,1)S(1)} %copy-done.4, f32[2048,512]{1,0:T(8,128)S(1)} %get-tuple-element.24), kind=kOutput, calls=%fused_computation.14 | convolution fusion | flops 2157445120 | bytes 9437184 | tf_op jit(solution)/shard_map/dot_general | solution.py:24
  88.5 3.3 %convolution_convert_fusion.3.g_up_ref = bf16[1024,512]{1,0:T(8,128)(2,1)} fusion(bf16[2048,1024]{1,0:T(8,128)(2,1)S(1)} %copy-done.3, bf16[2048,512]{1,0:T(8,128)(2,1)S(1)} %get-tuple-element.23), kind=kOutput, calls=%fused_computation.15 | convolution fusion | flops 2148007936 | bytes 7340032 | tf_op jit(solution)/shard_map/dot_general | solution.py:24
  91.8 0.0 copy-start.5
  91.8 4.3 %convolution_convert_fusion.back_ref = bf16[2048,1024]{1,0:T(8,128)(2,1)} fusion(bf16[2048,512]{1,0:T(8,128)(2,1)S(1)} %get-tuple-element.23, bf16[1024,512]{1,0:T(8,128)(2,1)S(1)} %copy-done.6), kind=kOutput, calls=%fused_computation.10 | convolution fusion | flops 2149580800 | bytes 7340032 | tf_op jit(solution)/shard_map/dot_general | solution.py:580
  96.2 0.0 copy-done.5
  96.2 4.8 %convolution_convert_fusion.1.branch_ref = bf16[2048,1024]{1,0:T(8,128)(2,1)} fusion(bf16[512,1024]{1,0:T(8,128)(2,1)S(1)} %copy-done.5, f32[2048,512]{1,0:T(8,128)S(1)} %get-tuple-element.24), kind=kOutput, calls=%fused_computation.11 | convolution fusion | flops 2159017984 | bytes 9437184 | tf_op jit(solution)/shard_map/dot_general | solution.py:579
  100.9 102.5 %scatter_all.1 = (bf16[128,1024]{1,0:T(8,128)(2,1)}, f32[128,1024]{1,0:T(8,128)}, f32[2,1024]{1,0:T(2,128)}, bf16[256,2048]{1,0:T(8,128)(2,1)}, bf16[2048,256]{1,0:T(8,128)(2,1)}) custom-call(bf16[2048,1024]{1,0:T(8,128)(2,1)} %convolution_convert_fusion.1.branch_ref, bf16[2048,1024]{1,0:T(8,128)(2,1)} %convolution_convert_fusion.back_ref, ...), custom_call_target="tpu_custom_call" | custom-call | tf_op jit(solution)/shard_map/scatter_all/pallas_call | solution.py:586
  203.5 0.0 copy-start.1
  203.5 0.0 copy-start
  203.5 0.0 copy-start.2
  203.5 2.9 %convert_multiply_fusion.1 = f32[256,2048]{1,0:T(8,128)} fusion(bf16[256,2048]{1,0:T(8,128)(2,1)} %get-tuple-element.20), kind=kLoop, calls=%fused_computation.13 | loop fusion | flops 1048576 | bytes 3145728 | tf_op jit(solution)/shard_map/mul | solution.py:613
  206.3 2.7 %convert_multiply_fusion = f32[2048,256]{1,0:T(8,128)} fusion(bf16[2048,256]{1,0:T(8,128)(2,1)} %get-tuple-element.21), kind=kLoop, calls=%fused_computation.12 | loop fusion | flops 1048576 | bytes 3145728 | tf_op jit(solution)/shard_map/mul | solution.py:614
  209.1 0.0 copy-done.1
  209.1 0.7 copy.16
  209.8 0.0 copy-done
  209.8 0.8 copy.17
  210.6 0.0 copy-done.2
  210.6 0.6 copy.18
  (2 shorter events, 0.0 us)
Async XLA Ops:
  74.0 5.0 %copy-start.3 = (bf16[2048,1024]{1,0:T(8,128)(2,1)S(1)}, bf16[2048,1024]{1,0:T(8,128)(2,1)}, u32[]{:S(2)}) copy-start(bf16[2048,1024]{1,0:T(8,128)(2,1)} %get-tuple-element.14) | copy-start | bytes 12582916
  74.0 5.0 %copy-start.6 = (bf16[1024,512]{1,0:T(8,128)(2,1)S(1)}, bf16[1024,512]{1,0:T(8,128)(2,1)}, u32[]{:S(2)}) copy-start(bf16[1024,512]{1,0:T(8,128)(2,1)} %get-tuple-element.15) | copy-start | bytes 3145732
  79.1 6.0 %copy-start.4 = (bf16[2048,1024]{1,0:T(8,128)(2,1)S(1)}, bf16[2048,1024]{1,0:T(8,128)(2,1)}, u32[]{:S(2)}) copy-start(bf16[2048,1024]{1,0:T(8,128)(2,1)} %get-tuple-element.17) | copy-start | bytes 12582916
  91.8 4.3 %copy-start.5 = (bf16[512,1024]{1,0:T(8,128)(2,1)S(1)}, bf16[512,1024]{1,0:T(8,128)(2,1)}, u32[]{:S(2)}) copy-start(bf16[512,1024]{1,0:T(8,128)(2,1)} %get-tuple-element.16) | copy-start | bytes 3145732
  203.5 5.6 %copy-start.1 = (bf16[128,1024]{1,0:T(8,128)(2,1)S(1)}, bf16[128,1024]{1,0:T(8,128)(2,1)}, u32[]{:S(2)}) copy-start(bf16[128,1024]{1,0:T(8,128)(2,1)} %get-tuple-element.30) | copy-start | bytes 786436
  203.5 6.3 %copy-start = (f32[128,1024]{1,0:T(8,128)S(1)}, f32[128,1024]{1,0:T(8,128)}, u32[]{:S(2)}) copy-start(f32[128,1024]{1,0:T(8,128)} %get-tuple-element.31) | copy-start | bytes 1572868
  203.5 7.1 %copy-start.2 = (f32[2,1024]{1,0:T(2,128)S(1)}, f32[2,1024]{1,0:T(2,128)}, u32[]{:S(2)}) copy-start(f32[2,1024]{1,0:T(2,128)} %get-tuple-element.34) | copy-start | bytes 24580

commit v2 on v1

--- a/solution.py
+++ b/solution.py
@@ -126,17 +126,17 @@
 
 def gather_kernel(
     n_groups, n_tensor, n_dp,
-    normed_ref, grad_ref, w_up_ref, w_down_ref,
+    first_ref, grad_ref, w_up_ref, w_down_ref, gain_ref, bias_ref,
     normed_all, grad_all, up_ref, down_ref,
-    local_sem, line_send, line_recv, column_send, column_recv,
+    own_normed, local_sem, line_send, line_recv, column_send, column_recv,
     weight_send, weight_recv, share_send, share_recv,
 ):
     group, tensor, dp = (lax.axis_index(name) for name in ("groups", "tensor", "dp"))
     bits = n_tensor.bit_length() - 1
-    rows = normed_ref.shape[0]
+    rows = first_ref.shape[0]
     depth = w_up_ref.shape[0]
     units = w_up_ref.shape[1] // n_dp
-    inputs, outputs = (normed_ref, grad_ref), (normed_all, grad_all)
+    outputs = (normed_all, grad_all)
     line_sems, column_sems = (line_send, line_recv), (column_send, column_recv)
     weight_sems, share_sems = (weight_send, weight_recv), (share_send, share_recv)
 
@@ -162,7 +162,7 @@
             source, target = dp - (distance - 1), dp + 1
         else:
             source, target = dp + (distance - 1), dp - 1
-        src = inputs[a] if distance == 1 else block(a, 0, source)
+        src = grad_ref if a == 1 and distance == 1 else block(a, 0, source)
         return remote(src, block(a, 0, source), line_sems, (a, side, distance), {"dp": target})
 
     def line_send_conditions(side, distance):
@@ -172,7 +172,7 @@
 
     def column_copy(a, mask, k, bit):
         source, _ = place(k)
-        src = inputs[a] if mask == 0 and k == 0 else block(a, mask, source)
+        src = grad_ref if a == 1 and mask == 0 and k == 0 else block(a, mask, source)
         return remote(
             src, block(a, mask, source), column_sems, (a, mask | 1 << bit, k),
             {"tensor": flipped(tensor, 1 << bit, bits)},
@@ -224,28 +224,39 @@
 
     greet(n_groups, n_dp, bits, group, tensor, dp)
     order = [0] + [k for s in range(1, n_dp) for k in (s, s + n_dp - 1)]
-    for a in range(2):
+    def send_own(a):
         for side in range(2):
-            guarded(line_send_conditions(side, 1), lambda a=a, side=side: line_copy(a, side, 1).start())
+            guarded(
+                line_send_conditions(side, 1), lambda side=side: line_copy(a, side, 1).start()
+            )
         pass_on(a, 0, 0)
+
+    send_own(1)
     for s in range(1, n_dp):
         for kind in range(2):
             weight_copy(kind, s).start()
     local = [
-        pltpu.make_async_copy(inputs[a], block(a, 0, dp), local_sem.at[a]) for a in range(2)
-    ]
-    local.append(
+        pltpu.make_async_copy(grad_ref, block(1, 0, dp), local_sem.at[1]),
         pltpu.make_async_copy(
             w_up_ref.at[:, span(dp, units)], up_ref.at[span(dp, depth), :], local_sem.at[2]
-        )
-    )
-    local.append(
+        ),
         pltpu.make_async_copy(
             w_down_ref.at[span(dp, units), :], down_ref.at[:, span(dp, depth)], local_sem.at[3]
-        )
-    )
+        ),
+    ]
     for copy in local:
         copy.start()
+
+    @pl.loop(0, rows // 16)
+    def _(i):
+        cut = pl.ds(pl.multiple_of(i * 16, 16), 16)
+        standard, _ = standardize(first_ref[cut, :])
+        own_normed[cut, :] = (standard * gain_ref[...] + bias_ref[...]).astype(own_normed.dtype)
+
+    settle = pltpu.make_async_copy(own_normed, block(0, 0, dp), local_sem.at[0])
+    settle.start()
+    settle.wait()
+    send_own(0)
 
     through = [m for m in range(1, n_tensor) if next_bits(m)]
     final = [m for m in range(1, n_tensor) if not next_bits(m)]
@@ -314,9 +325,10 @@
 
 def scatter_kernel(
     n_groups, n_tensor, n_dp, grad_scale,
-    branch_ref, back_ref, g_up_ref, g_down_ref, first_ref, second_ref, grad_ref, gain_ref,
+    hidden_ref, pre_ref, up_ref, down_ref, g_up_ref, g_down_ref,
+    first_ref, second_ref, grad_ref, gain_ref,
     second_in_ref, grad_first_ref, grad_norm_ref, up_out, down_out,
-    fold, right, left, stat_line, stat_fold, local_sem,
+    partials, fold, right, left, stat_line, stat_fold, local_sem,
     fold_send, fold_recv, line_send, line_recv, grads_send, grads_recv,
     stat_send, stat_recv, pair_send, pair_recv,
 ):
@@ -325,7 +337,6 @@
     rows, width = first_ref.shape
     units = g_up_ref.shape[1]
     depth = g_up_ref.shape[0] // n_dp
-    partials = (branch_ref, back_ref)
     fold_sems, line_sems = (fold_send, fold_recv), (line_send, line_recv)
     grads_sems, stat_sems, pair_sems = (
         (grads_send, grads_recv), (stat_send, stat_recv), (pair_send, pair_recv),
@@ -350,7 +361,7 @@
 
     def current(a, bit, mask, b):
         if bit == 0:
-            return partials[a].at[span(flipped(tensor, mask, bits) * n_dp + b, rows), :]
+            return partials.at[a, mask, b]
         return fold.at[a, slots[bit - 1, mask], b]
 
     def fold_copy(a, bit, mask, b):
@@ -384,13 +395,8 @@
     def kept_masks(bit):
         return sorted(range(0, n_tensor, 2 << bit), reverse=True)
 
-    for mask in sent_masks(0):
-        for b in range(n_dp):
-            for a in range(2):
-                fold_copy(a, 0, mask, b).start()
     for s in range(1, n_dp):
-        for kind in range(2):
-            grads_copy(kind, s).start()
+        grads_copy(0, s).start()
     local = [
         pltpu.make_async_copy(
             g_up_ref.at[span(dp, depth), :], up_out.at[:, span(dp, units)], local_sem.at[0]
@@ -401,14 +407,48 @@
     ]
     for copy in local:
         copy.start()
-    for bit in range(bits):
+
+    way = 2 * ((2 * dp) // n_dp) - 1
+
+    def multiply(mask, b):
+        cut = span(flipped(tensor, mask, bits) * n_dp + b, rows)
+        partials[0, mask, b] = jnp.dot(
+            hidden_ref[cut, :], down_ref[...], preferred_element_type=jnp.float32
+        ).astype(partials.dtype)
+        partials[1, mask, b] = lax.dot_general(
+            pre_ref[cut, :], up_ref[...], (((1,), (1,)), ((), ())),
+            preferred_element_type=jnp.float32,
+        ).astype(partials.dtype)
+
+    def folded(bit, mask, b):
+        for a in range(2):
+            fold_arrival(a, bit, mask, b).wait_recv()
+            add_into(fold.at[a, slots[bit, mask], b], current(a, bit, mask, b))
+            if bit + 1 < bits and mask in sent_masks(bit + 1):
+                fold_copy(a, bit + 1, mask, b).start()
+
+    for mask in sent_masks(0):
+        @pl.loop(0, n_dp)
+        def _(i, mask=mask):
+            b = (dp + way * (1 + i) + n_dp) % n_dp
+            multiply(mask, b)
+            for a in range(2):
+                fold_copy(a, 0, mask, b).start()
+
+        @pl.loop(0, n_dp)
+        def _(i, mask=mask):
+            b = (dp + way * (1 + i) + n_dp) % n_dp
+            multiply(mask - 1, b)
+            folded(0, mask - 1, b)
+
+    for bit in range(1, bits - 1):
         for mask in kept_masks(bit):
-            for b in range(n_dp):
-                for a in range(2):
-                    fold_arrival(a, bit, mask, b).wait_recv()
-                    add_into(fold.at[a, slots[bit, mask], b], current(a, bit, mask, b))
-                    if bit + 1 < bits and mask in sent_masks(bit + 1):
-                        fold_copy(a, bit + 1, mask, b).start()
+            for i in range(n_dp):
+                folded(bit, mask, (dp + way * (1 + i) + n_dp) % n_dp)
+
+    def finish(b):
+        if bits > 1:
+            folded(bits - 1, 0, b)
 
     last = slots[bits - 1, 0]
     moving = (right, left)
@@ -432,19 +472,24 @@
         return remote(here, here, line_sems, (a, side, s), line_peer(side))
 
     for s in range(n_dp - 1, 0, -1):
-        for a in range(2):
-            for side in range(2):
-                @pl.when(jnp.logical_and(line_conditions(side, s), jnp.logical_not(behind(side))))
-                def _(a=a, side=side, s=s):
+        for side in range(2):
+            @pl.when(jnp.logical_and(line_conditions(side, s), jnp.logical_not(behind(side))))
+            def _(side=side, s=s):
+                finish(dp + s if side == 0 else dp - s)
+                for a in range(2):
                     line_copy(a, side, s, False).start()
 
-                if s <= n_dp - 2:
-                    @pl.when(jnp.logical_and(line_conditions(side, s), behind(side)))
-                    def _(a=a, side=side, s=s):
-                        target = dp + s if side == 0 else dp - s
+            if s <= n_dp - 2:
+                @pl.when(jnp.logical_and(line_conditions(side, s), behind(side)))
+                def _(side=side, s=s):
+                    target = dp + s if side == 0 else dp - s
+                    finish(target)
+                    for a in range(2):
                         line_arrival(a, side, s).wait_recv()
                         add_into(moving[side].at[a, s], fold.at[a, last, target])
                         line_copy(a, side, s, True).start()
+        grads_copy(1, s).start()
+    finish(dp)
 
     for a in range(2):
         for side in range(2):
@@ -550,7 +595,7 @@
     bits = n_tensor.bit_length() - 1
     half = jnp.bfloat16
     grad_scale = tokens ** (-0.5)
-    _, _, own_normed = normalize(first_out, norm_gain, norm_bias)
+    gain, bias = norm_gain.reshape(1, -1), norm_bias.reshape(1, -1)
     normed, grad_all, up, down = pl.pallas_call(
         functools.partial(gather_kernel, n_groups, n_tensor, n_dp),
         out_shape=(
@@ -559,16 +604,16 @@
             jax.ShapeDtypeStruct((width, units), half),
             jax.ShapeDtypeStruct((units, width), half),
         ),
-        in_specs=[VMEM] * 4,
+        in_specs=[VMEM] * 6,
         out_specs=(ANY,) * 4,
-        scratch_shapes=[DMA((4,))]
+        scratch_shapes=[pltpu.VMEM((rows, width), half), DMA((4,))]
         + [DMA((2, 2, n_dp))] * 2
         + [DMA((2, n_tensor, 2 * n_dp - 1))] * 2
         + [DMA((2, n_dp))] * 2
         + [DMA((2, n_dp, n_groups))] * 2,
         compiler_params=pltpu.CompilerParams(collective_id=0, has_side_effects=True),
         name="gather_all",
-    )(own_normed, grad_second, w_up, w_down)
+    )(first_out, grad_second, w_up, w_down, gain, bias)
 
     preact = jnp.dot(normed, up, preferred_element_type=jnp.float32)
     hidden = jax.nn.gelu(preact).astype(half)
@@ -576,10 +621,6 @@
         grad_all, down, (((1,), (1,)), ((), ())), preferred_element_type=jnp.float32
     )
     grad_pre = jax.vjp(jax.nn.gelu, preact)[1](grad_hidden)[0].astype(half)
-    branch = jnp.dot(hidden, down, preferred_element_type=jnp.float32).astype(half)
-    back = lax.dot_general(
-        grad_pre, up, (((1,), (1,)), ((), ())), preferred_element_type=jnp.float32
-    ).astype(half)
     g_down = contract_tokens(hidden, grad_all).astype(half)
     g_up = contract_tokens(normed, grad_pre).astype(half)
 
@@ -592,9 +633,10 @@
             jax.ShapeDtypeStruct((w_up.shape[0], w_up.shape[1]), half),
             jax.ShapeDtypeStruct((w_down.shape[0], w_down.shape[1]), half),
         ),
-        in_specs=[VMEM] * 8,
+        in_specs=[VMEM] * 10,
         out_specs=(VMEM,) * 3 + (ANY,) * 2,
         scratch_shapes=[
+            pltpu.VMEM((2, n_tensor, n_dp, rows, width), half),
             pltpu.VMEM((2, n_tensor - 1, n_dp, rows, width), half),
             pltpu.VMEM((2, n_dp - 1, rows, width), half),
             pltpu.VMEM((2, n_dp - 1, rows, width), half),
@@ -609,7 +651,7 @@
         + [DMA((bits,))] * 2,
         compiler_params=pltpu.CompilerParams(collective_id=1, has_side_effects=True),
         name="scatter_all",
-    )(branch, back, g_up, g_down, first_out, second_out, grad_first, norm_gain.reshape(1, -1))
+    )(hidden, grad_pre, up, down, g_up, g_down, first_out, second_out, grad_first, gain)
     grad_up = up_out.astype(jnp.float32) * grad_scale
     grad_down = down_out.astype(jnp.float32) * grad_scale
     return second_in, grad_first_in, grad_up, grad_down, grad_norm

time: 211 us -> 196 us (0.929)
  matrix products: 26.8 us -> 16.9 us
  other arithmetic: 9.77 us -> 5.6 us
    dot_general x2 -> x0, matrix products: 9.07 us -> none  [the longest x1 4.76 us: spread_body(): jnp.dot(hidden, down, preferred_element_type=jnp.float32).astype(half)]
    pallas_call x1, Pallas kernels: 103 us -> 94.4 us  [spread_body(): pl.pallas_call(functools.partial(scatter_kernel, n_groups, n_tensor, n_dp...]
    pallas_call x1, Pallas kernels: 69.2 us -> 76 us  [spread_body(): pl.pallas_call(functools.partial(gather_kernel, n_groups, n_tensor, n_dp)...]
    reduce_sum x2 -> x0, other arithmetic: 2.24 us -> none  [the longest x1 1.17 us: normalize(): jnp.mean(centred * centred, axis=-1, keepdims=True) + epsilon]
where the time goes in v2:
time: 196 us
  Pallas kernels  170 us (87%)
  matrix products  16.9 us (9%)
  other arithmetic  5.6 us (3%)
  local copies, waits for them, and re-layouts  2.13 us (1%)
    pallas_call x1, Pallas kernels, spread_body(): pl.pallas_call(functools.partial(scatter_kernel, n_groups, n_tensor, n_dp...  94.4 us
    pallas_call x1, Pallas kernels, spread_body(): pl.pallas_call(functools.partial(gather_kernel, n_groups, n_tensor, n_dp)...  76 us
    dot_general x2, matrix products, contract_tokens(): lax.dot_general(left_rows, right_rows, (((0,), (0,)), ((), ())), preferre...  6.72 us
    dot_general x1, matrix products, spread_body(): preact = jnp.dot(normed, up, preferred_element_type=jnp.float32)  5.07 us
    dot_general x1, matrix products, spread_body(): lax.dot_general(grad_all, down, (((1,), (1,)), ((), ())), preferred_eleme...  5.06 us

profile of v2, /device:TPU:0, one launch (start us, length us, event | category | flops | bytes accessed | tf_op | source)
XLA Modules:
  0.0 195.7 jit_solution(15966572578320643865)
XLA Ops:
  0.6 76.0 %gather_all.1 = (bf16[2048,1024]{1,0:T(8,128)(2,1)}, bf16[2048,1024]{1,0:T(8,128)(2,1)}, bf16[1024,512]{1,0:T(8,128)(2,1)}, bf16[512,1024]{1,0:T(8,128)(2,1)}) custom-call(bf16[128,1024]{1,0:T(8,128)(2,1)} %first_ref.3, bf16[128,1024]{1,0:T(8,128)(2,1)} %grad_ref.2, bf16[256,2048]{1,0:T(8,128)(2,1)} %w_up_ref.1, bf16[2048,256]{1,0:T(8,128)(2,1)} %w_down_ref.1, ...), custom_call_target="tpu_custom_call" | custom-call | tf_op jit(solution)/shard_map/gather_all/pallas_call | solution.py:599
  76.6 0.0 copy-start.2
  76.6 0.0 copy-start.6
  76.6 5.1 %fusion.7 = f32[2048,512]{1,0:T(8,128)S(1)} fusion(bf16[2048,1024]{1,0:T(8,128)(2,1)} %get-tuple-element.16, bf16[512,1024]{1,0:T(8,128)(2,1)} %get-tuple-element.17.down_ref), kind=kOutput, calls=%fused_computation.14 | convolution fusion | flops 2147483648 | bytes 9437184 | tf_op jit(solution)/shard_map/dot_general | solution.py:620
  81.7 0.0 copy-done.2
  81.7 0.0 copy-done.6
  81.7 0.0 copy-start.7
  81.7 5.1 %fusion.6 = (bf16[2048,512]{1,0:T(8,128)(2,1)S(1)}, bf16[2048,512]{1,0:T(8,128)(2,1)S(1)}) fusion(f32[2048,512]{1,0:T(8,128)S(1)} %fusion.7, bf16[2048,1024]{1,0:T(8,128)(2,1)S(1)} %copy-done.6, bf16[1024,512]{1,0:T(8,128)(2,1)S(1)} %copy-done.2), kind=kOutput, calls=%fused_computation.8 | convolution fusion | flops 2170552320 | bytes 13631488 | tf_op jit(solution)/shard_map/dot_general | solution.py:618
  86.8 0.0 copy-start.1
  86.8 0.0 copy-start
  86.8 0.0 copy-done.7
  86.8 3.4 %convolution_convert_fusion.g_down_ref = bf16[512,1024]{1,0:T(8,128)(2,1)} fusion(bf16[2048,512]{1,0:T(8,128)(2,1)S(1)} %get-tuple-element.24.hidden_ref, bf16[2048,1024]{1,0:T(8,128)(2,1)S(1)} %copy-done.7), kind=kOutput, calls=%fused_computation.12 | convolution fusion | flops 2148007936 | bytes 7340032 | tf_op jit(solution)/shard_map/dot_general | solution.py:24
  90.2 0.0 copy-done.1
  90.2 0.0 copy-done
  90.2 3.3 %convolution_convert_fusion.1.g_up_ref = bf16[1024,512]{1,0:T(8,128)(2,1)} fusion(bf16[2048,1024]{1,0:T(8,128)(2,1)S(1)} %copy-done.6, bf16[2048,512]{1,0:T(8,128)(2,1)S(1)} %get-tuple-element.23.pre_ref), kind=kOutput, calls=%fused_computation.13 | convolution fusion | flops 2148007936 | bytes 7340032 | tf_op jit(solution)/shard_map/dot_general | solution.py:24
  93.6 94.4 %scatter_all.1 = (bf16[128,1024]{1,0:T(8,128)(2,1)}, f32[128,1024]{1,0:T(8,128)}, f32[2,1024]{1,0:T(2,128)}, bf16[256,2048]{1,0:T(8,128)(2,1)}, bf16[2048,256]{1,0:T(8,128)(2,1)}) custom-call(bf16[2048,512]{1,0:T(8,128)(2,1)} %copy-done.1, bf16[2048,512]{1,0:T(8,128)(2,1)} %copy-done, bf16[1024,512]{1,0:T(8,128)(2,1)} %get-tuple-element.15.up_ref, ...), custom_call_target="tpu_custom_call" | custom-call | tf_op jit(solution)/shard_map/scatter_all/pallas_call | solution.py:627
  187.9 0.0 copy-start.4
  187.9 0.0 copy-start.3
  188.0 0.0 copy-start.5
  188.0 2.9 %convert_multiply_fusion.1 = f32[256,2048]{1,0:T(8,128)} fusion(bf16[256,2048]{1,0:T(8,128)(2,1)} %get-tuple-element.20), kind=kLoop, calls=%fused_computation.11 | loop fusion | flops 1048576 | bytes 3145728 | tf_op jit(solution)/shard_map/mul | solution.py:655
  190.8 2.7 %convert_multiply_fusion = f32[2048,256]{1,0:T(8,128)} fusion(bf16[2048,256]{1,0:T(8,128)(2,1)} %get-tuple-element.21), kind=kLoop, calls=%fused_computation.10 | loop fusion | flops 1048576 | bytes 3145728 | tf_op jit(solution)/shard_map/mul | solution.py:656
  193.6 0.0 copy-done.4
  193.6 0.7 copy.16
  194.3 0.0 copy-done.3
  194.3 0.8 copy.17
  195.1 0.0 copy-done.5
  195.1 0.6 copy.18
Async XLA Ops:
  76.6 5.1 %copy-start.2 = (bf16[1024,512]{1,0:T(8,128)(2,1)S(1)}, bf16[1024,512]{1,0:T(8,128)(2,1)}, u32[]{:S(2)}) copy-start(bf16[1024,512]{1,0:T(8,128)(2,1)} %get-tuple-element.15.up_ref) | copy-start | bytes 3145732
  76.6 5.1 %copy-start.6 = (bf16[2048,1024]{1,0:T(8,128)(2,1)S(1)}, bf16[2048,1024]{1,0:T(8,128)(2,1)}, u32[]{:S(2)}) copy-start(bf16[2048,1024]{1,0:T(8,128)(2,1)} %get-tuple-element.14) | copy-start | bytes 12582916
  81.7 5.1 %copy-start.7 = (bf16[2048,1024]{1,0:T(8,128)(2,1)S(1)}, bf16[2048,1024]{1,0:T(8,128)(2,1)}, u32[]{:S(2)}) copy-start(bf16[2048,1024]{1,0:T(8,128)(2,1)} %get-tuple-element.16) | copy-start | bytes 12582916
  86.8 3.4 %copy-start.1 = (bf16[2048,512]{1,0:T(8,128)(2,1)}, bf16[2048,512]{1,0:T(8,128)(2,1)S(1)}, u32[]{:S(2)}) copy-start(bf16[2048,512]{1,0:T(8,128)(2,1)S(1)} %get-tuple-element.24.hidden_ref) | copy-start | bytes 6291460
  86.8 3.4 %copy-start = (bf16[2048,512]{1,0:T(8,128)(2,1)}, bf16[2048,512]{1,0:T(8,128)(2,1)S(1)}, u32[]{:S(2)}) copy-start(bf16[2048,512]{1,0:T(8,128)(2,1)S(1)} %get-tuple-element.23.pre_ref) | copy-start | bytes 6291460
  187.9 5.6 %copy-start.4 = (bf16[128,1024]{1,0:T(8,128)(2,1)S(1)}, bf16[128,1024]{1,0:T(8,128)(2,1)}, u32[]{:S(2)}) copy-start(bf16[128,1024]{1,0:T(8,128)(2,1)} %get-tuple-element.30) | copy-start | bytes 786436
  187.9 6.3 %copy-start.3 = (f32[128,1024]{1,0:T(8,128)S(1)}, f32[128,1024]{1,0:T(8,128)}, u32[]{:S(2)}) copy-start(f32[128,1024]{1,0:T(8,128)} %get-tuple-element.31) | copy-start | bytes 1572868
  188.0 7.1 %copy-start.5 = (f32[2,1024]{1,0:T(2,128)S(1)}, f32[2,1024]{1,0:T(2,128)}, u32[]{:S(2)}) copy-start(f32[2,1024]{1,0:T(2,128)} %get-tuple-element.34) | copy-start | bytes 24580

commit v3 on v2

--- a/solution.py
+++ b/solution.py
@@ -2,6 +2,7 @@
 
 import jax
 import jax.numpy as jnp
+import numpy as np
 from jax import lax
 from jax.experimental import pallas as pl
 from jax.experimental.pallas import tpu as pltpu
@@ -124,8 +125,8 @@
     )
 
 
-def gather_kernel(
-    n_groups, n_tensor, n_dp,
+def gather_tokens(
+    n_groups, n_tensor, n_dp, use,
     first_ref, grad_ref, w_up_ref, w_down_ref, gain_ref, bias_ref,
     normed_all, grad_all, up_ref, down_ref,
     own_normed, local_sem, line_send, line_recv, column_send, column_recv,
@@ -232,9 +233,6 @@
         pass_on(a, 0, 0)
 
     send_own(1)
-    for s in range(1, n_dp):
-        for kind in range(2):
-            weight_copy(kind, s).start()
     local = [
         pltpu.make_async_copy(grad_ref, block(1, 0, dp), local_sem.at[1]),
         pltpu.make_async_copy(
@@ -257,6 +255,9 @@
     settle.start()
     settle.wait()
     send_own(0)
+    for s in range(1, n_dp):
+        for kind in range(2):
+            weight_copy(kind, s).start()
 
     through = [m for m in range(1, n_tensor) if next_bits(m)]
     final = [m for m in range(1, n_tensor) if not next_bits(m)]
@@ -295,15 +296,25 @@
                 share_copy(kind, s, h).start()
     for k in done[n_dp - 1]:
         relay(k)
-    for k in order:
-        for a in range(2):
-            for mask in final:
-                guarded([place(k)[1]], lambda a=a, mask=mask, k=k: column_arrival(a, mask, k).wait_recv())
+    for copy in local:
+        copy.wait()
+    for s in range(1, n_dp):
+        for kind in range(2):
+            for h in range(1, n_groups):
+                share_arrival(kind, s, h).wait_recv()
+    for mask in [0] + through:
+        use(mask)
+    for mask in final:
+        for k in order:
+            for a in range(2):
+                guarded(
+                    [place(k)[1]], lambda a=a, mask=mask, k=k: column_arrival(a, mask, k).wait_recv()
+                )
+        use(mask)
     for s in range(1, n_dp):
         for kind in range(2):
             weight_copy(kind, s).wait_send()
             for h in range(1, n_groups):
-                share_arrival(kind, s, h).wait_recv()
                 share_copy(kind, s, h).wait_send()
     for a in range(2):
         for side in range(2):
@@ -319,12 +330,10 @@
                         [place(k)[1]],
                         lambda a=a, mask=mask, k=k, bit=bit: column_copy(a, mask, k, bit).wait_send(),
                     )
-    for copy in local:
-        copy.wait()
-
-
-def scatter_kernel(
-    n_groups, n_tensor, n_dp, grad_scale,
+
+
+def scatter_sums(
+    n_groups, n_tensor, n_dp, grad_scale, weight_block,
     hidden_ref, pre_ref, up_ref, down_ref, g_up_ref, g_down_ref,
     first_ref, second_ref, grad_ref, gain_ref,
     second_in_ref, grad_first_ref, grad_norm_ref, up_out, down_out,
@@ -335,8 +344,8 @@
     group, tensor, dp = (lax.axis_index(name) for name in ("groups", "tensor", "dp"))
     bits = n_tensor.bit_length() - 1
     rows, width = first_ref.shape
-    units = g_up_ref.shape[1]
-    depth = g_up_ref.shape[0] // n_dp
+    units = g_up_ref.shape[2]
+    depth = g_up_ref.shape[1]
     fold_sems, line_sems = (fold_send, fold_recv), (line_send, line_recv)
     grads_sems, stat_sems, pair_sems = (
         (grads_send, grads_recv), (stat_send, stat_recv), (pair_send, pair_recv),
@@ -349,9 +358,9 @@
     def grads_copy(kind, s):
         target = (dp + s) % n_dp
         if kind == 0:
-            src, dst = g_up_ref.at[span(target, depth), :], up_out.at[:, span(dp, units)]
+            src, dst = g_up_ref.at[target], up_out.at[:, span(dp, units)]
         else:
-            src, dst = g_down_ref.at[:, span(target, depth)], down_out.at[span(dp, units), :]
+            src, dst = g_down_ref.at[target], down_out.at[span(dp, units), :]
         return remote(src, dst, grads_sems, (kind, s), {"dp": target})
 
     def grads_arrival(kind, s):
@@ -386,8 +395,6 @@
                 ref[cut, :].astype(jnp.float32) + other[cut, :].astype(jnp.float32)
             ).astype(ref.dtype)
 
-    greet(n_groups, n_dp, bits, group, tensor, dp)
-
     def sent_masks(bit):
         masks = [m for m in range(n_tensor) if m % (1 << bit) == 0 and m >> bit & 1]
         return sorted(masks, reverse=True)
@@ -395,15 +402,19 @@
     def kept_masks(bit):
         return sorted(range(0, n_tensor, 2 << bit), reverse=True)
 
-    for s in range(1, n_dp):
+    @pl.loop(1, n_dp)
+    def _(s):
+        weight_block(0, (dp + s) % n_dp)
         grads_copy(0, s).start()
+
+    @pl.loop(1, n_dp + 1)
+    def _(s):
+        weight_block(1, (dp + s) % n_dp)
+
+    weight_block(0, dp)
     local = [
-        pltpu.make_async_copy(
-            g_up_ref.at[span(dp, depth), :], up_out.at[:, span(dp, units)], local_sem.at[0]
-        ),
-        pltpu.make_async_copy(
-            g_down_ref.at[:, span(dp, depth)], down_out.at[span(dp, units), :], local_sem.at[1]
-        ),
+        pltpu.make_async_copy(g_up_ref.at[dp], up_out.at[:, span(dp, units)], local_sem.at[0]),
+        pltpu.make_async_copy(g_down_ref.at[dp], down_out.at[span(dp, units), :], local_sem.at[1]),
     ]
     for copy in local:
         copy.start()
@@ -582,6 +593,65 @@
     return centred * inv_std, inv_std
 
 
+def fused_kernel(
+    n_groups, n_tensor, n_dp, grad_scale,
+    first_ref, second_ref, grad_first_in_ref, grad_ref, w_up_ref, w_down_ref, gain_ref, bias_ref,
+    second_in_ref, grad_first_ref, grad_norm_ref, up_out, down_out,
+    normed_all, grad_all, up_ref, down_ref, hidden_ref, pre_ref, g_up_ref, g_down_ref,
+    *scratch,
+):
+    tensor = lax.axis_index("tensor")
+    bits = n_tensor.bit_length() - 1
+    column = first_ref.shape[0] * n_dp
+    chunk = column // 2
+    depth = g_up_ref.shape[1]
+    gather_count = 10
+
+    def use(mask):
+        base = flipped(tensor, mask, bits)
+
+        @pl.loop(0, column // chunk)
+        def _(i):
+            cut = span(base * (column // chunk) + i, chunk)
+            preact = jnp.dot(
+                normed_all[cut, :], up_ref[...], preferred_element_type=jnp.float32
+            )
+            grad_hidden = lax.dot_general(
+                grad_all[cut, :], down_ref[...], (((1,), (1,)), ((), ())),
+                preferred_element_type=jnp.float32,
+            )
+            root = (2.0 / np.pi) ** 0.5
+            square = preact * preact
+            bend = jnp.tanh(root * (preact + 0.044715 * (square * preact)))
+            gate = 0.5 * (1.0 + bend)
+            hidden_ref[cut, :] = (preact * gate).astype(hidden_ref.dtype)
+            slope = gate + (0.5 * preact) * (1.0 - bend * bend) * (
+                root * (1.0 + 3.0 * 0.044715 * square)
+            )
+            pre_ref[cut, :] = (grad_hidden * slope).astype(pre_ref.dtype)
+
+    def weight_block(kind, target):
+        cut = span(target, depth)
+        if kind == 0:
+            g_up_ref[target] = contract_tokens(normed_all[:, cut], pre_ref[...]).astype(g_up_ref.dtype)
+        else:
+            g_down_ref[target] = contract_tokens(hidden_ref[...], grad_all[:, cut]).astype(
+                g_down_ref.dtype
+            )
+
+    gather_tokens(
+        n_groups, n_tensor, n_dp, use,
+        first_ref, grad_ref, w_up_ref, w_down_ref, gain_ref, bias_ref,
+        normed_all, grad_all, up_ref, down_ref, *scratch[:gather_count],
+    )
+    scatter_sums(
+        n_groups, n_tensor, n_dp, grad_scale, weight_block,
+        hidden_ref, pre_ref, up_ref, down_ref, g_up_ref, g_down_ref,
+        first_ref, second_ref, grad_first_in_ref, gain_ref,
+        second_in_ref, grad_first_ref, grad_norm_ref, up_out, down_out, *scratch[gather_count:],
+    )
+
+
 ANY = pl.BlockSpec(memory_space=pl.ANY)
 VMEM = pl.BlockSpec(memory_space=pltpu.VMEM)
 DMA = pltpu.SemaphoreType.DMA
@@ -596,46 +666,34 @@
     half = jnp.bfloat16
     grad_scale = tokens ** (-0.5)
     gain, bias = norm_gain.reshape(1, -1), norm_bias.reshape(1, -1)
-    normed, grad_all, up, down = pl.pallas_call(
-        functools.partial(gather_kernel, n_groups, n_tensor, n_dp),
-        out_shape=(
-            jax.ShapeDtypeStruct((tokens, width), half),
-            jax.ShapeDtypeStruct((tokens, width), half),
-            jax.ShapeDtypeStruct((width, units), half),
-            jax.ShapeDtypeStruct((units, width), half),
-        ),
-        in_specs=[VMEM] * 6,
-        out_specs=(ANY,) * 4,
-        scratch_shapes=[pltpu.VMEM((rows, width), half), DMA((4,))]
-        + [DMA((2, 2, n_dp))] * 2
-        + [DMA((2, n_tensor, 2 * n_dp - 1))] * 2
-        + [DMA((2, n_dp))] * 2
-        + [DMA((2, n_dp, n_groups))] * 2,
-        compiler_params=pltpu.CompilerParams(collective_id=0, has_side_effects=True),
-        name="gather_all",
-    )(first_out, grad_second, w_up, w_down, gain, bias)
-
-    preact = jnp.dot(normed, up, preferred_element_type=jnp.float32)
-    hidden = jax.nn.gelu(preact).astype(half)
-    grad_hidden = lax.dot_general(
-        grad_all, down, (((1,), (1,)), ((), ())), preferred_element_type=jnp.float32
-    )
-    grad_pre = jax.vjp(jax.nn.gelu, preact)[1](grad_hidden)[0].astype(half)
-    g_down = contract_tokens(hidden, grad_all).astype(half)
-    g_up = contract_tokens(normed, grad_pre).astype(half)
-
+    depth = w_up.shape[0]
     second_in, grad_first_in, grad_norm, up_out, down_out = pl.pallas_call(
-        functools.partial(scatter_kernel, n_groups, n_tensor, n_dp, grad_scale),
+        functools.partial(fused_kernel, n_groups, n_tensor, n_dp, grad_scale),
         out_shape=(
             jax.ShapeDtypeStruct((rows, width), half),
             jax.ShapeDtypeStruct((rows, width), jnp.float32),
             jax.ShapeDtypeStruct((2, width), jnp.float32),
-            jax.ShapeDtypeStruct((w_up.shape[0], w_up.shape[1]), half),
-            jax.ShapeDtypeStruct((w_down.shape[0], w_down.shape[1]), half),
+            jax.ShapeDtypeStruct(w_up.shape, half),
+            jax.ShapeDtypeStruct(w_down.shape, half),
         ),
-        in_specs=[VMEM] * 10,
+        in_specs=[VMEM] * 8,
         out_specs=(VMEM,) * 3 + (ANY,) * 2,
         scratch_shapes=[
+            pltpu.VMEM((tokens, width), half),
+            pltpu.VMEM((tokens, width), half),
+            pltpu.VMEM((width, units), half),
+            pltpu.VMEM((units, width), half),
+            pltpu.VMEM((tokens, units), half),
+            pltpu.VMEM((tokens, units), half),
+            pltpu.VMEM((n_dp, depth, units), half),
+            pltpu.VMEM((n_dp, units, depth), half),
+        ]
+        + [pltpu.VMEM((rows, width), half), DMA((4,))]
+        + [DMA((2, 2, n_dp))] * 2
+        + [DMA((2, n_tensor, 2 * n_dp - 1))] * 2
+        + [DMA((2, n_dp))] * 2
+        + [DMA((2, n_dp, n_groups))] * 2
+        + [
             pltpu.VMEM((2, n_tensor, n_dp, rows, width), half),
             pltpu.VMEM((2, n_tensor - 1, n_dp, rows, width), half),
             pltpu.VMEM((2, n_dp - 1, rows, width), half),
@@ -649,9 +707,11 @@
         + [DMA((2, n_dp))] * 2
         + [DMA((n_dp,))] * 2
         + [DMA((bits,))] * 2,
-        compiler_params=pltpu.CompilerParams(collective_id=1, has_side_effects=True),
-        name="scatter_all",
-    )(hidden, grad_pre, up, down, g_up, g_down, first_out, second_out, grad_first, gain)
+        compiler_params=pltpu.CompilerParams(
+            collective_id=0, has_side_effects=True, vmem_limit_bytes=60 << 20
+        ),
+        name="spread_backward",
+    )(first_out, second_out, grad_first, grad_second, w_up, w_down, gain, bias)
     grad_up = up_out.astype(jnp.float32) * grad_scale
     grad_down = down_out.astype(jnp.float32) * grad_scale
     return second_in, grad_first_in, grad_up, grad_down, grad_norm
@@ -664,6 +724,7 @@
     fits = (
         n_tensor > 1
         and n_dp > 1
+        and n_dp % 2 == 0
         and n_tensor & (n_tensor - 1) == 0
         and w_up.shape[1] % (n_dp * n_groups * 128) == 0
         and w_up.shape[0] % (n_groups * 128) == 0

time: 196 us -> 168 us (0.86)
  matrix products: 16.9 us -> 0 us
  Pallas kernels: 170 us -> 161 us
    dot_general x4 -> x0, matrix products: 16.9 us -> none  [the longest x2 6.72 us: contract_tokens(): lax.dot_general(left_rows, right_rows, (((0,), (0,)), ((), ())), preferre...]
    pallas_call x2 -> x1, Pallas kernels: 170 us -> 161 us  [spread_body(): pl.pallas_call(functools.partial(fused_kernel, n_groups, n_tensor, n_dp,...]
where the time goes in v3:
time: 168 us
  Pallas kernels  161 us (96%)
  other arithmetic  4.39 us (3%)
  local copies, waits for them, and re-layouts  2.11 us (1%)
    pallas_call x1, Pallas kernels, spread_body(): pl.pallas_call(functools.partial(fused_kernel, n_groups, n_tensor, n_dp,...  161 us

profile of v3, /device:TPU:0, one launch (start us, length us, event | category | flops | bytes accessed | tf_op | source)
XLA Modules:
  0.0 167.8 jit_solution(9616201336427600147)
XLA Ops:
  0.6 160.7 %spread_backward.1 = (bf16[128,1024]{1,0:T(8,128)(2,1)}, f32[128,1024]{1,0:T(8,128)}, f32[2,1024]{1,0:T(2,128)}, bf16[256,2048]{1,0:T(8,128)(2,1)}, bf16[2048,256]{1,0:T(8,128)(2,1)}) custom-call(bf16[128,1024]{1,0:T(8,128)(2,1)} %first_ref.1, bf16[128,1024]{1,0:T(8,128)(2,1)} %second_ref.1, bf16[128,1024]{1,0:T(8,128)(2,1)} %grad_first_in_ref.1, ...), custom_call_target="tpu_custom_call" | custom-call | tf_op jit(solution)/shard_map/spread_backward/pallas_call | solution.py:670
  161.3 0.0 copy-start
  161.3 2.9 %convert_multiply_fusion.1 = f32[256,2048]{1,0:T(8,128)} fusion(bf16[256,2048]{1,0:T(8,128)(2,1)} %get-tuple-element.12), kind=kLoop, calls=%fused_computation.1 | loop fusion | flops 1048576 | bytes 3145728 | tf_op jit(solution)/shard_map/mul | solution.py:715
  164.2 0.0 copy-done
  164.2 0.0 copy-start.2
  164.2 0.0 copy-start.1
  164.2 0.0 copy-start.3
  164.2 1.5 convert_multiply_fusion
  165.7 0.0 copy-done.2
  165.7 0.7 copy.16
  166.4 0.0 copy-done.1
  166.4 0.8 copy.17
  167.2 0.0 copy-done.3
  167.2 0.6 copy.18
Async XLA Ops:
  161.3 2.9 %copy-start = (bf16[2048,256]{1,0:T(8,128)(2,1)S(1)}, bf16[2048,256]{1,0:T(8,128)(2,1)}, u32[]{:S(2)}) copy-start(bf16[2048,256]{1,0:T(8,128)(2,1)} %get-tuple-element.13) | copy-start | bytes 3145732
  164.2 1.5 copy-start.2
  164.2 2.2 %copy-start.1 = (f32[128,1024]{1,0:T(8,128)S(1)}, f32[128,1024]{1,0:T(8,128)}, u32[]{:S(2)}) copy-start(f32[128,1024]{1,0:T(8,128)} %get-tuple-element.21) | copy-start | bytes 1572868
  164.2 3.0 %copy-start.3 = (f32[2,1024]{1,0:T(2,128)S(1)}, f32[2,1024]{1,0:T(2,128)}, u32[]{:S(2)}) copy-start(f32[2,1024]{1,0:T(2,128)} %get-tuple-element.24) | copy-start | bytes 24580

commit v4 on v3

--- a/solution.py
+++ b/solution.py
@@ -407,18 +407,6 @@
         weight_block(0, (dp + s) % n_dp)
         grads_copy(0, s).start()
 
-    @pl.loop(1, n_dp + 1)
-    def _(s):
-        weight_block(1, (dp + s) % n_dp)
-
-    weight_block(0, dp)
-    local = [
-        pltpu.make_async_copy(g_up_ref.at[dp], up_out.at[:, span(dp, units)], local_sem.at[0]),
-        pltpu.make_async_copy(g_down_ref.at[dp], down_out.at[span(dp, units), :], local_sem.at[1]),
-    ]
-    for copy in local:
-        copy.start()
-
     way = 2 * ((2 * dp) // n_dp) - 1
 
     def multiply(mask, b):
@@ -483,6 +471,7 @@
         return remote(here, here, line_sems, (a, side, s), line_peer(side))
 
     for s in range(n_dp - 1, 0, -1):
+        weight_block(1, (dp + s) % n_dp)
         for side in range(2):
             @pl.when(jnp.logical_and(line_conditions(side, s), jnp.logical_not(behind(side))))
             def _(side=side, s=s):
@@ -500,6 +489,14 @@
                         add_into(moving[side].at[a, s], fold.at[a, last, target])
                         line_copy(a, side, s, True).start()
         grads_copy(1, s).start()
+    weight_block(0, dp)
+    weight_block(1, dp)
+    local = [
+        pltpu.make_async_copy(g_up_ref.at[dp], up_out.at[:, span(dp, units)], local_sem.at[0]),
+        pltpu.make_async_copy(g_down_ref.at[dp], down_out.at[span(dp, units), :], local_sem.at[1]),
+    ]
+    for copy in local:
+        copy.start()
     finish(dp)
 
     for a in range(2):

time: 168 us -> 164 us (0.976)
  Pallas kernels: 161 us -> 157 us
    pallas_call x1, Pallas kernels: 161 us -> 157 us  [spread_body(): pl.pallas_call(functools.partial(fused_kernel, n_groups, n_tensor, n_dp,...]
where the time goes in v4:
time: 164 us
  Pallas kernels  157 us (96%)
  other arithmetic  4.39 us (3%)
  local copies, waits for them, and re-layouts  2.11 us (1%)
    pallas_call x1, Pallas kernels, spread_body(): pl.pallas_call(functools.partial(fused_kernel, n_groups, n_tensor, n_dp,...  157 us

profile of v4, /device:TPU:0, one launch (start us, length us, event | category | flops | bytes accessed | tf_op | source)
XLA Modules:
  0.0 164.0 jit_solution(12689409481628773706)
XLA Ops:
  0.6 156.8 %spread_backward.1 = (bf16[128,1024]{1,0:T(8,128)(2,1)}, f32[128,1024]{1,0:T(8,128)}, f32[2,1024]{1,0:T(2,128)}, bf16[256,2048]{1,0:T(8,128)(2,1)}, bf16[2048,256]{1,0:T(8,128)(2,1)}) custom-call(bf16[128,1024]{1,0:T(8,128)(2,1)} %first_ref.1, bf16[128,1024]{1,0:T(8,128)(2,1)} %second_ref.1, bf16[128,1024]{1,0:T(8,128)(2,1)} %grad_first_in_ref.1, ...), custom_call_target="tpu_custom_call" | custom-call | tf_op jit(solution)/shard_map/spread_backward/pallas_call | solution.py:667
  157.5 0.0 copy-start
  157.5 2.9 %convert_multiply_fusion.1 = f32[256,2048]{1,0:T(8,128)} fusion(bf16[256,2048]{1,0:T(8,128)(2,1)} %get-tuple-element.12), kind=kLoop, calls=%fused_computation.1 | loop fusion | flops 1048576 | bytes 3145728 | tf_op jit(solution)/shard_map/mul | solution.py:712
  160.4 0.0 copy-done
  160.4 0.0 copy-start.2
  160.4 0.0 copy-start.1
  160.4 0.0 copy-start.3
  160.4 1.5 convert_multiply_fusion
  161.9 0.0 copy-done.2
  161.9 0.7 copy.16
  162.6 0.0 copy-done.1
  162.6 0.8 copy.17
  163.4 0.0 copy-done.3
  163.4 0.6 copy.18
Async XLA Ops:
  157.5 2.9 %copy-start = (bf16[2048,256]{1,0:T(8,128)(2,1)S(1)}, bf16[2048,256]{1,0:T(8,128)(2,1)}, u32[]{:S(2)}) copy-start(bf16[2048,256]{1,0:T(8,128)(2,1)} %get-tuple-element.13) | copy-start | bytes 3145732
  160.4 1.5 copy-start.2
  160.4 2.2 %copy-start.1 = (f32[128,1024]{1,0:T(8,128)S(1)}, f32[128,1024]{1,0:T(8,128)}, u32[]{:S(2)}) copy-start(f32[128,1024]{1,0:T(8,128)} %get-tuple-element.21) | copy-start | bytes 1572868
  160.4 3.0 %copy-start.3 = (f32[2,1024]{1,0:T(2,128)S(1)}, f32[2,1024]{1,0:T(2,128)}, u32[]{:S(2)}) copy-start(f32[2,1024]{1,0:T(2,128)} %get-tuple-element.24) | copy-start | bytes 24580

commit v5 on v4

--- a/solution.py
+++ b/solution.py
@@ -255,9 +255,18 @@
     settle.start()
     settle.wait()
     send_own(0)
-    for s in range(1, n_dp):
+
+    def send_weights(s):
         for kind in range(2):
             weight_copy(kind, s).start()
+
+    def share_weights(s):
+        for kind in range(2):
+            weight_arrival(kind, s).wait_recv()
+            for h in range(1, n_groups):
+                share_copy(kind, s, h).start()
+
+    send_weights(1)
 
     through = [m for m in range(1, n_tensor) if next_bits(m)]
     final = [m for m in range(1, n_tensor) if not next_bits(m)]
@@ -288,12 +297,13 @@
                     pass_on(a, 0, k)
 
                 guarded([place(k)[1]], action)
+        if s < n_dp - 1:
+            send_weights(s + 1)
         for k in done[s - 1]:
             relay(k)
-        for kind in range(2):
-            weight_arrival(kind, s).wait_recv()
-            for h in range(1, n_groups):
-                share_copy(kind, s, h).start()
+        if s > 1:
+            share_weights(s - 1)
+    share_weights(n_dp - 1)
     for k in done[n_dp - 1]:
         relay(k)
     for copy in local:

time: 164 us -> 166 us (1.012)
  Pallas kernels: 157 us -> 159 us
    pallas_call x1, Pallas kernels: 157 us -> 159 us  [spread_body(): pl.pallas_call(functools.partial(fused_kernel, n_groups, n_tensor, n_dp,...]
where the time goes in v5:
time: 166 us
  Pallas kernels  159 us (96%)
  other arithmetic  4.39 us (3%)
  local copies, waits for them, and re-layouts  2.11 us (1%)
    pallas_call x1, Pallas kernels, spread_body(): pl.pallas_call(functools.partial(fused_kernel, n_groups, n_tensor, n_dp,...  159 us

profile of v5, /device:TPU:0, one launch (start us, length us, event | category | flops | bytes accessed | tf_op | source)
XLA Modules:
  0.0 166.0 jit_solution(17658351882627082626)
XLA Ops:
  0.6 158.9 %spread_backward.1 = (bf16[128,1024]{1,0:T(8,128)(2,1)}, f32[128,1024]{1,0:T(8,128)}, f32[2,1024]{1,0:T(2,128)}, bf16[256,2048]{1,0:T(8,128)(2,1)}, bf16[2048,256]{1,0:T(8,128)(2,1)}) custom-call(bf16[128,1024]{1,0:T(8,128)(2,1)} %first_ref.1, bf16[128,1024]{1,0:T(8,128)(2,1)} %second_ref.1, bf16[128,1024]{1,0:T(8,128)(2,1)} %grad_first_in_ref.1, ...), custom_call_target="tpu_custom_call" | custom-call | tf_op jit(solution)/shard_map/spread_backward/pallas_call | solution.py:677
  159.5 0.0 copy-start
  159.5 2.9 %convert_multiply_fusion.1 = f32[256,2048]{1,0:T(8,128)} fusion(bf16[256,2048]{1,0:T(8,128)(2,1)} %get-tuple-element.12), kind=kLoop, calls=%fused_computation.1 | loop fusion | flops 1048576 | bytes 3145728 | tf_op jit(solution)/shard_map/mul | solution.py:722
  162.4 0.0 copy-done
  162.4 0.0 copy-start.2
  162.4 0.0 copy-start.1
  162.4 0.0 copy-start.3
  162.4 1.5 convert_multiply_fusion
  163.9 0.0 copy-done.2
  163.9 0.7 copy.16
  164.6 0.0 copy-done.1
  164.7 0.8 copy.17
  165.4 0.0 copy-done.3
  165.4 0.6 copy.18
Async XLA Ops:
  159.5 2.9 %copy-start = (bf16[2048,256]{1,0:T(8,128)(2,1)S(1)}, bf16[2048,256]{1,0:T(8,128)(2,1)}, u32[]{:S(2)}) copy-start(bf16[2048,256]{1,0:T(8,128)(2,1)} %get-tuple-element.13) | copy-start | bytes 3145732
  162.4 1.5 copy-start.2
  162.4 2.2 %copy-start.1 = (f32[128,1024]{1,0:T(8,128)S(1)}, f32[128,1024]{1,0:T(8,128)}, u32[]{:S(2)}) copy-start(f32[128,1024]{1,0:T(8,128)} %get-tuple-element.21) | copy-start | bytes 1572868
  162.4 3.0 %copy-start.3 = (f32[2,1024]{1,0:T(2,128)S(1)}, f32[2,1024]{1,0:T(2,128)}, u32[]{:S(2)}) copy-start(f32[2,1024]{1,0:T(2,128)} %get-tuple-element.24) | copy-start | bytes 24580
